TPU v7x, 32 devices: a whole 2x2x4 slice. The times are simulated.
32 devices in a mesh: freq: 4 (over y, core), tcol: 8 (over z, x).
Axes of the slice: x: 2, y: 2, z: 4, core: 2. Of those that a mesh axis runs over, the one named last changes fastest.
Arguments:
- data: bfloat16 [4, 2, 4096, 128], P('freq', None, 'tcol'), may hold values from -6 to 6
- left_factor: bfloat16 [4, 2, 4096, 256], P('freq', None, 'tcol'), may hold values from -0.25 to 0.25
- right_factor: bfloat16 [4, 2, 4096, 256], P('freq', None, 'tcol'), may hold values from -0.1875 to 0.1875
- ranks: int32 [4, 8, 8], P('freq'), may hold values from 1 to 32
- freq_index: int32 [4], P('freq'), may hold values from 0 to 229
Outputs:
- wavefield: float32 [4, 2, 4096, 128], P('freq', None, 'tcol')
- residual: float32 [4, 2, 4096, 128], P('freq', None, 'tcol')
Inputs may be any that keep to these rules, and one draw needn't show every extreme that they name: `ranks`: the rank of each tile; factor columns at or beyond it are not part of the kernel.
All inputs are finite; a program needn't handle non-finite values.
Results may differ from a plain program's by a relative error of at most 0.006.
Values may be sent and summed in bfloat16 or wider, within the bound.
No kernel may reach another device: no remote copies, remote signals or barrier semaphores. Data moves between devices by JAX's collectives and lax.ppermute only.
A program may use at most 64 MiB of HBM per device.

v0:
```python
import functools

import jax
import jax.numpy as jnp
from jax import lax
from jax.experimental import pallas as pl
from jax.experimental.pallas import tpu as pltpu
from jax.sharding import PartitionSpec as P


RIDE = 16
LATE = 4
EARLY = 9
VMEM = pl.BlockSpec(memory_space=pltpu.VMEM)
SMEM = pl.BlockSpec(memory_space=pltpu.SMEM)
HBM = pl.BlockSpec(memory_space=pltpu.HBM)
F32 = jnp.float32
BF16 = jnp.bfloat16


def dot(a, b):
    return jnp.dot(a, b, preferred_element_type=F32)


def dot_t(a, b):
    return lax.dot_general(a, b, (((0,), (0,)), ((), ())), preferred_element_type=F32)


def side(real, imag):
    return jnp.concatenate([real, imag], axis=1)


def split(value):
    high = value.astype(BF16)
    return high, (value - high.astype(F32)).astype(BF16)


def unpack(ref, rank):
    n = ref.shape[0]
    real = ref[:, 0:rank, :].reshape(n * rank, ref.shape[2])
    imag = ref[:, rank : 2 * rank, :].reshape(n * rank, ref.shape[2])
    return real, imag


def fields(ref, rank):
    return side(*unpack(ref, rank)).astype(F32)


def send(out_ref, value, rank):
    s = out_ref.shape[2]
    for p in range(out_ref.shape[0]):
        rows = value[p * rank : (p + 1) * rank].astype(BF16)
        out_ref[p, 0:rank, :] = rows[:, :s]
        out_ref[p, rank : 2 * rank, :] = rows[:, s:]


def ride(out_ref, rows, rank):
    rows = rows + [jnp.zeros_like(rows[0])] * (RIDE - len(rows))
    block = jnp.concatenate(rows, axis=0).astype(BF16)
    for p in range(out_ref.shape[0]):
        out_ref[p, 2 * rank : 2 * rank + RIDE, :] = block


def ridden(ref, rank):
    total = ref[0, 2 * rank : 2 * rank + RIDE, :].astype(F32)
    for p in range(1, ref.shape[0]):
        total = total + ref[p, 2 * rank : 2 * rank + RIDE, :].astype(F32)
    return total


def inner(a, b):
    both = jnp.sum(a * b, axis=0, keepdims=True)
    s = both.shape[1] // 2
    return both[:, :s] + both[:, s:]


def twice(row):
    return jnp.concatenate([row, row], axis=1)


def ratio(top, bottom):
    safe = bottom > 0
    return jnp.where(safe, top / jnp.where(safe, bottom, 1.0), 0.0)


def apply_gram(hi_ref, lo_ref, real, imag):
    vector = jnp.concatenate([side(real, imag), side(-imag, real)], axis=0)
    return dot(hi_ref[...], vector) + dot(lo_ref[...], vector)


def make_gram(factor_ref, hi_ref, lo_ref, limits):
    real, imag = factor_ref[0], factor_ref[1]
    width = real.shape[1]
    rank = width // len(limits)
    level = lax.broadcasted_iota(jnp.int32, (rank, width), 0)

    def put(value, place):
        for p, limit in enumerate(limits):
            rows = slice(p * rank, (p + 1) * rank)
            high, low = split(jnp.where(level < limit, value[rows], 0.0))
            hi_ref[rows, place : place + width] = high
            lo_ref[rows, place : place + width] = low

    put(dot_t(real, real) + dot_t(imag, imag), 0)
    put(dot_t(real, imag) - dot_t(imag, real), width)


def start_kernel(
    rank, here_ref, mine_ref, ranks_hbm, freq_hbm, data_hbm, left_hbm, right_hbm,
    right_ref, back_ref, sums_ref, out_ref, uhi_ref, ulo_ref, vhi_ref, vlo_ref,
    ranks_ref, freq_ref, data_ref, left_ref, sem
):
    n = out_ref.shape[0]
    s = out_ref.shape[2]
    pairs = [
        (left_hbm, left_ref), (data_hbm, data_ref), (ranks_hbm, ranks_ref),
        (freq_hbm, freq_ref), (right_hbm, right_ref),
    ]
    copies = [
        pltpu.make_async_copy(source, target, sem.at[k])
        for k, (source, target) in enumerate(pairs)
    ]
    for copy in copies:
        copy.start()
    for copy in copies[:4]:
        copy.wait()
    here = here_ref[0]
    row_limits = [ranks_ref[here, p] for p in range(n)]
    column_limits = [ranks_ref[p, here] for p in range(n)]
    damping = 0.1 + 0.9 * freq_ref[0].astype(F32) / 229.0
    sums_ref[...] = jnp.full(sums_ref.shape, damping)
    real, imag = data_ref[0], data_ref[1]
    back = dot_t(left_ref[0], side(real, imag)) + dot_t(left_ref[1], side(imag, -real))
    level = lax.broadcasted_iota(jnp.int32, (rank, 2 * s), 0)
    back = jnp.concatenate(
        [
            jnp.where(level < limit, back[p * rank : (p + 1) * rank], 0.0)
            for p, limit in enumerate(row_limits)
        ],
        axis=0,
    )
    back_ref[...] = back
    send(out_ref, back, rank)
    make_gram(left_ref, uhi_ref, ulo_ref, row_limits)
    copies[4].wait()
    make_gram(right_ref, vhi_ref, vlo_ref, column_limits)


def column0(rank, b0_ref, hi_ref, lo_ref, g0_ref, sums_ref, out_ref):
    real, imag = unpack(b0_ref, rank)
    g0 = apply_gram(hi_ref, lo_ref, real, imag)
    g0_ref[...] = g0
    m00 = inner(side(real, imag).astype(F32), g0)
    sums_ref[0:1, :] = m00
    send(out_ref, g0, rank)
    ride(out_ref, [m00], rank)


def row0(rank, c0_ref, hi_ref, lo_ref, back_ref, sums_ref, out_ref):
    real, imag = unpack(c0_ref, rank)
    next0 = apply_gram(hi_ref, lo_ref, real, imag)
    c0 = side(real, imag).astype(F32)
    n00 = inner(c0, next0)
    sums_ref[0:1, :] = n00
    sums_ref[1:2, :] = inner(back_ref[...], c0)
    sums_ref[2:3, :] = ridden(c0_ref, rank)[0:1]
    send(out_ref, next0, rank)
    ride(out_ref, [n00], rank)


def column1(
    rank, b1_ref, b0_ref, hi_ref, lo_ref, g0_ref, n0_ref, g1_ref, sums_ref, out_ref
):
    real, imag = unpack(b1_ref, rank)
    theta0 = ratio(ridden(b1_ref, rank)[0:1], n0_ref[2:3, :])
    wide = twice(theta0)
    g1 = apply_gram(hi_ref, lo_ref, real, imag) - wide * g0_ref[...]
    b0 = fields(b0_ref, rank)
    b1 = side(real, imag).astype(F32) - wide * b0
    g1_ref[...] = g1
    m11 = inner(b1, g1)
    sums_ref[0:1, :] = m11
    sums_ref[1:2, :] = inner(b0, g1)
    sums_ref[2:3, :] = theta0
    send(out_ref, g1, rank)
    ride(out_ref, [m11], rank)


def row1(rank, c1_ref, c0_ref, hi_ref, lo_ref, back_ref, sums_ref, out_ref):
    real, imag = unpack(c1_ref, rank)
    next1 = apply_gram(hi_ref, lo_ref, real, imag)
    c1 = side(real, imag).astype(F32)
    n11 = inner(c1, next1)
    n01 = inner(fields(c0_ref, rank), next1)
    sums_ref[0:1, :] = n11
    sums_ref[1:2, :] = n01
    sums_ref[2:3, :] = inner(back_ref[...], c1)
    sums_ref[3:4, :] = ridden(c1_ref, rank)[0:1]
    send(out_ref, next1, rank)
    ride(out_ref, [n11, n01], rank)


def column2(
    rank, b2_ref, b0_ref, b1_ref, hi_ref, lo_ref, g0_ref, g1_ref,
    damp_ref, m0_ref, n0_ref, m1_ref, n1_ref, sums_ref, out_ref
):
    real, imag = unpack(b2_ref, rank)
    came = ridden(b2_ref, rank)
    theta1 = ratio(came[0:1], n1_ref[3:4, :])
    phi = ratio(came[1:2], n0_ref[2:3, :])
    wide1, wide0 = twice(theta1), twice(phi)
    g2 = apply_gram(hi_ref, lo_ref, real, imag) - wide1 * g1_ref[...] - wide0 * g0_ref[...]
    send(out_ref, g2, rank)
    b0 = fields(b0_ref, rank)
    b1 = fields(b1_ref, rank) - twice(m1_ref[2:3, :]) * b0
    b2 = side(real, imag).astype(F32) - wide1 * b1 - wide0 * b0
    sums_ref[0:1, :] = inner(b0, g2)
    sums_ref[1:2, :] = inner(b1, g2)
    sums_ref[2:3, :] = inner(b2, g2)
    sums_ref[3:4, :] = theta1
    sums_ref[4:5, :] = phi
    damping = damp_ref[0:1, :]
    known = [
        n0_ref[0:1, :] + damping * m0_ref[0:1, :],
        n1_ref[1:2, :] + damping * m1_ref[1:2, :],
        n1_ref[0:1, :] + damping * m1_ref[0:1, :],
        n0_ref[1:2, :],
        n1_ref[2:3, :],
    ]
    rest = [row - row.astype(BF16).astype(F32) for row in known]
    ride(out_ref, known + rest, rank)


def row2(
    rank, share, here_ref, c2_ref, c0_ref, c1_ref, hi_ref, lo_ref, back_ref,
    damp_ref, m1_ref, m2_ref, out_ref, table_ref
):
    real, imag = unpack(c2_ref, rank)
    next2 = apply_gram(hi_ref, lo_ref, real, imag)
    damping = damp_ref[0:1, :]
    came = ridden(c2_ref, rank)
    table_ref[0:5, :] = came[0:5] + came[5:10]
    table_ref[5:6, :] = m1_ref[2:3, :]
    table_ref[6:8, :] = m2_ref[3:5, :]
    table_ref[8:9, :] = damping
    rows = [
        inner(fields(c0_ref, rank), next2) + damping * m2_ref[0:1, :],
        inner(fields(c1_ref, rank), next2) + damping * m2_ref[1:2, :],
        inner(side(real, imag).astype(F32), next2) + damping * m2_ref[2:3, :],
        inner(back_ref[...], side(real, imag).astype(F32)),
        table_ref[pl.ds(here_ref[0] * share, share), :],
    ]
    more = out_ref.shape[1] - LATE - share
    if more:
        rows.append(jnp.zeros((more, real.shape[1]), F32))
    block = jnp.concatenate(rows, axis=0)
    for p in range(out_ref.shape[0]):
        out_ref[p] = block


def forms(h, u, g, p, position, size, axis):
    def times(v):
        return [sum(h[a][b] * v[b] for b in range(size)) for a in range(size)]

    def along(a, b):
        return jnp.sum(sum(x * y for x, y in zip(a, b)), axis=axis, keepdims=True)

    hg, hp, hx = times(g), times(p), times(position)
    rest = [u[a] - hx[a] for a in range(size)]
    return along(g, hg), along(p, hg), along(p, hp), along(g, rest), along(p, rest)


def descend(h, u, theta0, theta1, phi, damping, axis):
    one = jnp.ones_like(theta0)
    a11 = jnp.sum(h[0][0], axis=axis, keepdims=True)
    b1 = jnp.sum(u[0], axis=axis, keepdims=True)
    alpha = b1 / (1.1 * a11)
    p = [alpha * one]
    x = [alpha * one]
    for size in (2, 3):
        zero = jnp.zeros_like(one)
        x = x + [zero]
        p = p + [zero]
        if size == 2:
            g = [one - (theta0 + damping) * x[0], -x[0]]
        else:
            g = [
                one - (theta0 + damping) * x[0] - phi * x[1],
                -x[0] - (theta1 + damping) * x[1],
                -x[1],
            ]
        a11, a12, a22, b1, b2 = forms(h, u, g, p, x, size, axis)
        first, second = 1.1 * a11, 1.1 * a22
        determinant = first * second - a12 * a12
        alpha = (b1 * second - a12 * b2) / determinant
        beta = (first * b2 - a12 * b1) / determinant
        p = [alpha * g[a] + beta * p[a] for a in range(size)]
        x = [x[a] + p[a] for a in range(size)]
    return x


def finish_kernel(
    rank, nfreq, share, mine_ref, data_hbm, left_hbm, recv_ref, right_ref,
    b0_ref, b1_ref, b2_ref, c0_ref, c1_ref, c2_ref, wave_hbm, res_hbm,
    table_ref, mix_ref, wave_ref, res_ref, data_ref, left_ref, sem
):
    left_copy = pltpu.make_async_copy(left_hbm, left_ref, sem.at[2])
    data_copy = pltpu.make_async_copy(data_hbm, data_ref, sem.at[3])
    left_copy.start()
    data_copy.start()
    ntile = recv_ref.shape[0] // nfreq
    for f in range(nfreq):
        total = recv_ref[f * ntile]
        for t in range(1, ntile):
            total = total + recv_ref[f * ntile + t]
        table_ref[0:LATE, f, :] = total[0:LATE]
        for q in range(EARLY):
            place = LATE + q % share
            table_ref[LATE + q, f : f + 1, :] = recv_ref[f * ntile + q // share, place : place + 1]
    h = [[None] * 3 for _ in range(3)]
    places = [(0, 0, 2), (1, 1, 2), (2, 2, 2), (4, 0, 0), (5, 0, 1), (6, 1, 1)]
    for place, a, b in places:
        h[a][b] = h[b][a] = table_ref[place]
    u = [table_ref[7], table_ref[8], table_ref[3]]
    theta0, theta1, phi, damping = [table_ref[9 + a] for a in range(4)]
    x = descend(h, u, theta0, theta1, phi, damping, 0)
    mix_ref[0] = x[0] - theta0 * x[1] + (theta0 * theta1 - phi) * x[2]
    mix_ref[1] = x[1] - theta1 * x[2]
    mix_ref[2] = x[2]
    mix_ref[3] = x[0]
    mix_ref[4] = x[1]
    mix_ref[5] = x[2]
    row = pl.ds(mine_ref[0], 1)

    def combine(refs, offset):
        total = None
        for k, ref in enumerate(refs):
            scale = mix_ref[offset + k, row, :]
            real, imag = unpack(ref, rank)
            term = (scale * real.astype(F32), scale * imag.astype(F32))
            total = term if total is None else (total[0] + term[0], total[1] + term[1])
        return total

    def plain(factor_ref, real, imag):
        (rh, rl), (ih, il) = split(real), split(imag)
        first, second = factor_ref[0], factor_ref[1]
        return (
            dot(first, side(rh, ih)) + dot(second, side(-ih, rh))
            + dot(first, side(rl, il)) + dot(second, side(-il, rl))
        )

    s = wave_ref.shape[2]
    wave = plain(right_ref, *combine([b0_ref, b1_ref, b2_ref], 0))
    wave_ref[0] = wave[:, :s]
    wave_ref[1] = wave[:, s:]
    wave_copy = pltpu.make_async_copy(wave_ref, wave_hbm, sem.at[0])
    wave_copy.start()
    mixed = combine([c0_ref, c1_ref, c2_ref], 3)
    left_copy.wait()
    data_copy.wait()
    image = plain(left_ref, *mixed)
    res_ref[0] = data_ref[0].astype(F32) - image[:, :s]
    res_ref[1] = data_ref[1].astype(F32) - image[:, s:]
    res_copy = pltpu.make_async_copy(res_ref, res_hbm, sem.at[1])
    res_copy.start()
    wave_copy.wait()
    res_copy.wait()


def lane_limits(limits, rank, width):
    lane = lax.broadcasted_iota(jnp.int32, (1, width), 1)
    limit = jnp.zeros((1, width), jnp.int32)
    for p, value in enumerate(limits):
        limit = jnp.where(lane >= p * rank, value, limit)
    return (lax.rem(lane, rank) < limit).astype(F32)


def packed_gram(real, imag):
    width = real.shape[1]
    both = jnp.concatenate([real, imag], axis=0)
    upper = dot_t(both, both)
    lower = dot_t(real, imag) - dot_t(imag, real)
    row = lax.broadcasted_iota(jnp.int32, (width, width), 0)
    column = lax.broadcasted_iota(jnp.int32, (width, width), 1)
    return jnp.where(row <= column, upper, lower).astype(BF16)


def unpacked_gram(packed):
    width = packed.shape[1]
    here = packed.astype(F32)
    there = here.T
    row = lax.broadcasted_iota(jnp.int32, (width, width), 0)
    column = lax.broadcasted_iota(jnp.int32, (width, width), 1)
    real = jnp.where(row <= column, here, there)
    imag = jnp.where(row > column, here, jnp.where(row < column, -there, 0.0))
    return real.astype(BF16), imag.astype(BF16)


def direct_offsets(half):
    others = [k for k in range(1, half) if k != 2]
    return sorted(others, key=lambda k: (min(k, half - k), k))


def start_left(rank, n, here_ref, mine_ref, ranks_hbm, data_hbm, left_hbm, right_hbm, *refs):
    keep_ref, right_ref, ranks_ref, data_ref, left_ref, back_ref, sem = refs[-7:]
    half = n // 2
    direct = [0] + direct_offsets(half)
    packets, own = refs[: half - 1], refs[half - 1]
    pairs = [
        (left_hbm, left_ref), (data_hbm, data_ref), (ranks_hbm, ranks_ref),
        (right_hbm, right_ref),
    ]
    copies = [
        pltpu.make_async_copy(source, target, sem.at[k])
        for k, (source, target) in enumerate(pairs)
    ]
    for copy in copies:
        copy.start()
    for copy in copies[:3]:
        copy.wait()
    width = left_ref.shape[2]
    s = data_ref.shape[2]
    q = s // n
    here = here_ref[0]
    keep = lane_limits([ranks_ref[here, p] for p in range(n)], rank, width).astype(BF16)
    real, imag = left_ref[0] * keep, left_ref[1] * keep
    both = side(data_ref[0], data_ref[1])
    first, second = dot_t(both, real), dot_t(both, imag)
    back_ref[0] = (first[:s] + second[s:]).astype(BF16)
    back_ref[1] = (first[s:] - second[:s]).astype(BF16)
    gram = packed_gram(real, imag)
    for k, packet in zip(direct, packets):
        place = 4 * q if k == 1 else 0
        packet[place : place + width, :] = gram
    z, x = lax.div(here, 2), lax.rem(here, 2)
    for k in range(half):
        base = 2 * lax.rem(z + k, half)
        for block, target in enumerate([base + 1 - x, base + x]):
            rows = pl.ds(pl.multiple_of(target * q, q), q)
            if k == 2:
                out, place = packets[direct.index(1)], 2 * q * block
            elif k == 0 and block == 1:
                out, place = own, 0
            else:
                out, place = packets[direct.index(k)], width + 2 * q * block
                place += 4 * q if k == 1 else 0
            out[place : place + q, :] = back_ref[0, rows, :]
            out[place + q : place + 2 * q, :] = back_ref[1, rows, :]
    keep = lane_limits([ranks_ref[p, here] for p in range(n)], rank, width)
    keep_ref[...] = jnp.broadcast_to(keep, keep_ref.shape)
    copies[3].wait()


def start_right(right_ref, keep_ref, out_ref):
    keep = keep_ref[0:1, :].astype(BF16)
    out_ref[...] = packed_gram(right_ref[0] * keep, right_ref[1] * keep)


def swap_tiles(rank, source, target):
    n, rows, width = source.shape
    per = 128 // rank
    lane = lax.div(lax.broadcasted_iota(jnp.int32, (rows, 128), 1), rank)
    for g in range(n // per):
        for h in range(width // 128):
            ins = [source[per * g + a, :, 128 * h : 128 * h + 128] for a in range(per)]
            for b in range(per):
                out = None
                for a in range(per):
                    shift = (a - b) * rank % 128
                    piece = pltpu.roll(ins[a], shift, 1) if shift else ins[a]
                    out = piece if out is None else jnp.where(lane == a, piece, out)
                target[per * h + b, :, 128 * g : 128 * g + 128] = out


def apply_tiles(gram_ref, source, target):
    n, rows, _ = source.shape
    q = rows // 2
    for j in range(n):
        high, low = split(source[j])
        vector = jnp.concatenate([high, low], axis=0)
        real, imag = dot(vector, gram_ref[0, j]), dot(vector, gram_ref[1, j])
        real = real[:rows] + real[rows:]
        imag = imag[:rows] + imag[rows:]
        target[j, 0:q, :] = real[:q] + imag[q:]
        target[j, q:rows, :] = real[q:] - imag[:q]


def inner_tiles(first, second):
    n, rows, _ = first.shape
    total = first[0] * second[0]
    for j in range(1, n):
        total = total + first[j] * second[j]
    total = jnp.sum(total, axis=1, keepdims=True)
    return total[: rows // 2] + total[rows // 2 :]


def take_off(target, terms):
    scales = [jnp.concatenate([scale, scale], axis=0) for scale, _ in terms]
    for j in range(target.shape[0]):
        value = target[j]
        for scale, (_, other) in zip(scales, terms):
            value = value - scale * other[j]
        target[j] = value


def chain_kernel(
    rank, n, here_ref, freq_ref, *refs
):
    half = n // 2
    order = [0] + direct_offsets(half) + [2]
    lefts = [refs[:half], refs[half:n]]
    rights = [refs[n : n + half], refs[n + half : 2 * n]]
    own = refs[2 * n]
    b_ref, c_ref, stats_ref, left_ref, right_ref, one_ref, two_ref = refs[2 * n + 1 :]
    width = refs[0].shape[1]
    q = stats_ref.shape[0]
    here = here_ref[0]
    z, x = lax.div(here, 2), lax.rem(here, 2)
    for k in range(half):
        base = 2 * lax.rem(z + half - k, half)
        for other in range(2):
            ref = lefts[other][order.index(k)]
            at = pl.ds(base + (1 - x if other else x), 1)
            top = 4 * q if k == 2 or (k == 1 and not other) else 0
            grams = (ref[top : top + width, :], rights[other][order.index(k)][...])
            for packed, gram_ref in zip(grams, (left_ref, right_ref)):
                real, imag = unpacked_gram(packed)
                gram_ref[0, at] = real[None]
                gram_ref[1, at] = imag[None]
            start = (0 if k == 2 else top + width) + (0 if other else 2 * q)
            if k == 0 and not other:
                block = own[...]
            else:
                block = ref[start : start + 2 * q, :]
            one_ref[at] = block.astype(F32)[None]
    b0, b1, b2 = b_ref.at[0], b_ref.at[1], b_ref.at[2]
    c0, c1, c2 = c_ref.at[0], c_ref.at[1], c_ref.at[2]
    swap_tiles(rank, one_ref, b0)
    apply_tiles(right_ref, b0, two_ref)
    m00 = inner_tiles(b0, two_ref)
    swap_tiles(rank, two_ref, c0)
    apply_tiles(left_ref, c0, one_ref)
    n00 = inner_tiles(c0, one_ref)
    theta0 = ratio(n00, m00)
    swap_tiles(rank, one_ref, b1)
    take_off(b1, [(theta0, b0)])
    apply_tiles(right_ref, b1, two_ref)
    m11 = inner_tiles(b1, two_ref)
    m01 = inner_tiles(b0, two_ref)
    swap_tiles(rank, two_ref, c1)
    apply_tiles(left_ref, c1, one_ref)
    n11 = inner_tiles(c1, one_ref)
    n01 = inner_tiles(c0, one_ref)
    theta1 = ratio(n11, m11)
    phi = ratio(n01, m00)
    swap_tiles(rank, one_ref, b2)
    take_off(b2, [(theta1, b1), (phi, b0)])
    apply_tiles(right_ref, b2, two_ref)
    m02 = inner_tiles(b0, two_ref)
    m12 = inner_tiles(b1, two_ref)
    m22 = inner_tiles(b2, two_ref)
    swap_tiles(rank, two_ref, c2)
    apply_tiles(left_ref, c2, one_ref)
    n02 = inner_tiles(c0, one_ref)
    n12 = inner_tiles(c1, one_ref)
    n22 = inner_tiles(c2, one_ref)
    damping = 0.1 + 0.9 * freq_ref[0].astype(F32) / 229.0
    values = [
        n00 + damping * m00, n01 + damping * m01, n02 + damping * m02,
        n11 + damping * m11, n12 + damping * m12, n22 + damping * m22,
        m00, m01, m02, theta0, theta1, phi,
    ]
    lane = lax.broadcasted_iota(jnp.int32, stats_ref.shape, 1)
    block = jnp.full(stats_ref.shape, damping)
    for place, value in enumerate(values):
        block = jnp.where(lane == place, value, block)
    stats_ref[...] = block


def mix_kernel(stats_refs, b_ref, c_ref, out_ref):
    blocks = [ref[...] for ref in stats_refs]
    lane = lax.broadcasted_iota(jnp.int32, blocks[0].shape, 1)
    where_f = [lane == f for f in range(len(blocks))]

    def pick(place):
        value = jnp.zeros_like(blocks[0])
        for f, block in enumerate(blocks):
            shift = (f - place) % 128
            value = jnp.where(where_f[f], pltpu.roll(block, shift, 1) if shift else block, value)
        return value

    h = [[None] * 3 for _ in range(3)]
    for place, (a, b) in enumerate([(0, 0), (0, 1), (0, 2), (1, 1), (1, 2), (2, 2)]):
        h[a][b] = h[b][a] = pick(place)
    u = [pick(6), pick(7), pick(8)]
    theta0, theta1, phi, damping = pick(9), pick(10), pick(11), pick(12)
    x = descend(h, u, theta0, theta1, phi, damping, 1)
    n, rows, _ = b_ref.shape[1:]
    scales = []
    for value in x:
        own = jnp.sum(jnp.where(lane == 0, value, 0.0), axis=1, keepdims=True)
        scales.append(jnp.concatenate([own, own], axis=0))
    for j in range(n):
        for place, ref in enumerate((b_ref, c_ref)):
            value = scales[0] * ref[0, j] + scales[1] * ref[1, j] + scales[2] * ref[2, j]
            out_ref[j, place * rows : (place + 1) * rows, :] = value.astype(BF16)


def home_mix(nfreq, data_hbm, left_hbm, right_hbm, *refs):
    stats_refs = refs[:nfreq]
    b_ref, c_ref, out_ref, data_ref, left_ref, right_ref, sem = refs[nfreq:]
    pairs = [(right_hbm, right_ref), (left_hbm, left_ref), (data_hbm, data_ref)]
    copies = [
        pltpu.make_async_copy(source, target, sem.at[k])
        for k, (source, target) in enumerate(pairs)
    ]
    for copy in copies:
        copy.start()
    mix_kernel(stats_refs, b_ref, c_ref, out_ref)
    for copy in copies:
        copy.wait()


def dot_nt(a, b):
    return lax.dot_general(a, b, (((1,), (1,)), ((), ())), preferred_element_type=F32)


def home_kernel(
    recv_ref, data_ref, left_ref, right_ref, wave_hbm, res_hbm, wave_ref, res_ref, sem
):
    n, rows, width = recv_ref.shape
    q = rows // 4
    s = n * q

    def plain(factor_ref, place):
        real = recv_ref[:, place * q : (place + 1) * q, :].reshape(s, width)
        imag = recv_ref[:, (place + 1) * q : (place + 2) * q, :].reshape(s, width)
        both = jnp.concatenate([real, imag], axis=0)
        first, second = dot_nt(factor_ref[0], both), dot_nt(factor_ref[1], both)
        return first[:, :s] - second[:, s:], first[:, s:] + second[:, :s]

    wave_ref[0], wave_ref[1] = plain(right_ref, 0)
    wave_copy = pltpu.make_async_copy(wave_ref, wave_hbm, sem.at[0])
    wave_copy.start()
    real, imag = plain(left_ref, 2)
    res_ref[0] = data_ref[0].astype(F32) - real
    res_ref[1] = data_ref[1].astype(F32) - imag
    res_copy = pltpu.make_async_copy(res_ref, res_hbm, sem.at[1])
    res_copy.start()
    wave_copy.wait()
    res_copy.wait()


def by_source(data, left, right, ranks, freq_index, ntile, nfreq, here, mine):
    width = left.shape[2]
    rank = width // ntile
    s = data.shape[2]
    q = s // ntile
    half = ntile // 2
    room = (16 << 20) + 64 * width * width

    def like(value):
        return jax.ShapeDtypeStruct(value.shape, value.dtype)

    def call(kernel, specs, args, outs, scratch=(), target=VMEM):
        return pl.pallas_call(
            kernel,
            out_shape=outs,
            in_specs=specs,
            out_specs=[target] * len(outs),
            scratch_shapes=scratch,
            compiler_params=pltpu.CompilerParams(vmem_limit_bytes=room),
        )(*args)

    def along(shift):
        return [
            (2 * z + x, 2 * ((z + shift) % half) + x) for z in range(half) for x in range(2)
        ]

    across = [(t, t ^ 1) for t in range(ntile)]
    direct = direct_offsets(half)
    sizes = [width + (8 if k == 1 else 4) * q for k in direct]
    sizes = [width + 2 * q] + sizes + [2 * q]
    parts = call(
        functools.partial(start_left, rank, ntile), [SMEM] * 2 + [HBM] * 4,
        (here, mine, ranks, data, left, right),
        [jax.ShapeDtypeStruct((size, width), BF16) for size in sizes]
        + [jax.ShapeDtypeStruct((8, width), F32), like(right)],
        [
            pltpu.SMEM(ranks.shape, jnp.int32),
            pltpu.VMEM(data.shape, BF16),
            pltpu.VMEM(left.shape, BF16),
            pltpu.VMEM((2, s, width), BF16),
            pltpu.SemaphoreType.DMA((4,)),
        ],
    )
    (gram,) = call(
        start_right, [VMEM] * 2, (parts[-1], parts[-2]),
        [jax.ShapeDtypeStruct((width, width), BF16)],
    )

    def hop(value, pairs):
        return lax.ppermute(value, "tcol", pairs)

    lefts, rights = [parts[0]], [gram]
    cross = [hop(parts[0], across), hop(gram, across)]
    for place, k in enumerate(direct):
        first, second = parts[1 + place], gram
        if place:
            first, _ = lax.optimization_barrier((first, lefts[-1]))
            second, _ = lax.optimization_barrier((second, rights[-1]))
        lefts.append(hop(first, along(k)))
        rights.append(hop(second, along(k)))
    first, _ = lax.optimization_barrier((lefts[1], lefts[-1]))
    first = first[: width + 4 * q]
    second, _ = lax.optimization_barrier((rights[1], rights[-1]))
    lefts.append(hop(first, along(1)))
    rights.append(hop(second, along(1)))
    other_lefts, other_rights = cross[:1], cross[1:]
    for place in range(1, half):
        value = lefts[1][4 * q :] if place == 1 else lefts[place]
        other_lefts.append(hop(value, across))
        other_rights.append(hop(rights[place], across))
    packets = (*lefts, *other_lefts, *rights, *other_rights, parts[half - 1])
    vectors = jax.ShapeDtypeStruct((3, ntile, 2 * q, width), F32)
    grams = pltpu.VMEM((2, ntile, width, width), BF16)
    vector = pltpu.VMEM((ntile, 2 * q, width), F32)
    b, c, stats = call(
        functools.partial(chain_kernel, rank, ntile), [SMEM] * 2 + [VMEM] * len(packets),
        (here, freq_index, *packets),
        (vectors, vectors, jax.ShapeDtypeStruct((q, 128), F32)),
        [grams, grams, vector, vector],
    )
    gathered = [stats] + [
        lax.ppermute(stats, "freq", [(f, f ^ step) for f in range(nfreq)])
        for step in range(1, nfreq)
    ]
    out, data_in, left_in, right_in = call(
        functools.partial(home_mix, nfreq), [HBM] * 3 + [VMEM] * (nfreq + 2),
        (data, left, right, *gathered, b, c),
        (
            jax.ShapeDtypeStruct((ntile, 4 * q, width), BF16),
            like(data), like(left), like(right),
        ),
        [pltpu.SemaphoreType.DMA((3,))],
    )
    back = lax.all_to_all(out, "tcol", 0, 0, tiled=True)
    shape = jax.ShapeDtypeStruct(data.shape, F32)
    return call(
        home_kernel, [VMEM] * 4, (back, data_in, left_in, right_in),
        (shape, shape),
        [
            pltpu.VMEM(shape.shape, F32),
            pltpu.VMEM(shape.shape, F32),
            pltpu.SemaphoreType.DMA((2,)),
        ],
        HBM,
    )


def body(data, left_factor, right_factor, ranks, freq_index):
    ntile = lax.axis_size("tcol")
    nfreq = lax.axis_size("freq")
    here = lax.axis_index("tcol").reshape(1)
    mine = lax.axis_index("freq").reshape(1)
    data, left, right, ranks = data[0], left_factor[0], right_factor[0], ranks[0]
    data, left, right, ranks = [
        pltpu.with_memory_space_constraint(value, pltpu.HBM)
        for value in (data, left, right, ranks)
    ]
    width = left.shape[2]
    rank = width // ntile
    s = data.shape[2]
    fits = ntile % 2 == 0 and ntile >= 6 and s % (16 * ntile) == 0 and width % 128 == 0 and 128 % rank == 0
    if fits and nfreq & (nfreq - 1) == 0 and ntile * width * width <= 1 << 20:
        wave, res = by_source(data, left, right, ranks, freq_index, ntile, nfreq, here, mine)
        return wave[None], res[None]
    share = -(-EARLY // ntile)
    height = -(-(LATE + share) // 8) * 8
    field = jax.ShapeDtypeStruct((width, 2 * s), F32)
    sums = jax.ShapeDtypeStruct((8, s), F32)
    bare = jax.ShapeDtypeStruct((ntile, 2 * rank, s), BF16)
    message = jax.ShapeDtypeStruct((ntile, 2 * rank + RIDE, s), BF16)
    gram = jax.ShapeDtypeStruct((width, 2 * width), BF16)
    room = (8 << 20) + 24 * width * width

    def like(value):
        return jax.ShapeDtypeStruct(value.shape, value.dtype)

    def call(kernel, specs, args, outs, scratch=(), target=VMEM):
        return pl.pallas_call(
            functools.partial(kernel, rank),
            out_shape=outs,
            in_specs=specs,
            out_specs=[target] * len(outs),
            scratch_shapes=scratch,
            compiler_params=pltpu.CompilerParams(vmem_limit_bytes=room),
        )(*args)

    def step(kernel, args, outs):
        return call(kernel, [VMEM] * len(args), args, outs)

    def exchange(value):
        return lax.all_to_all(value, "tcol", 0, 0, tiled=True)

    vright, back, damp, out, uhi, ulo, vhi, vlo = call(
        start_kernel, [SMEM] * 2 + [HBM] * 5, (here, mine, ranks, freq_index, data, left, right),
        (like(right), field, sums, bare, gram, gram, gram, gram),
        [
            pltpu.SMEM(ranks.shape, jnp.int32),
            pltpu.SMEM(freq_index.shape, jnp.int32),
            pltpu.VMEM(data.shape, BF16),
            pltpu.VMEM(left.shape, BF16),
            pltpu.SemaphoreType.DMA((5,)),
        ],
    )
    b0 = exchange(out)
    g0, m0, out = step(column0, (b0, vhi, vlo), (field, sums, message))
    c0 = exchange(out)
    n0, out = step(row0, (c0, uhi, ulo, back), (sums, message))
    b1 = exchange(out)
    g1, m1, out = step(column1, (b1, b0, vhi, vlo, g0, n0), (field, sums, message))
    c1 = exchange(out)
    n1, out = step(row1, (c1, c0, uhi, ulo, back), (sums, message))
    b2 = exchange(out)
    m2, out = step(
        column2, (b2, b0, b1, vhi, vlo, g0, g1, damp, m0, n0, m1, n1), (sums, message)
    )
    c2 = exchange(out)
    args = (here, c2, c0, c1, uhi, ulo, back, damp, m1, m2)
    (out,) = call(
        lambda rank, *refs: row2(rank, share, *refs), [SMEM] + [VMEM] * 9, args,
        (jax.ShapeDtypeStruct((nfreq * ntile, height, s), F32),),
        [pltpu.VMEM((max(16, ntile * share), s), F32)],
    )
    everyone = lax.all_to_all(out, ("freq", "tcol"), 0, 0, tiled=True)
    shape = jax.ShapeDtypeStruct(data.shape, F32)
    wave, res = call(
        lambda rank, *refs: finish_kernel(rank, nfreq, share, *refs),
        [SMEM, HBM, HBM] + [VMEM] * 8,
        (mine, data, left, everyone, vright, b0, b1, b2, c0, c1, c2), (shape, shape),
        [
            pltpu.VMEM((LATE + EARLY, nfreq, s), F32),
            pltpu.VMEM((6, nfreq, s), F32),
            pltpu.VMEM(shape.shape, F32),
            pltpu.VMEM(shape.shape, F32),
            pltpu.VMEM(data.shape, BF16),
            pltpu.VMEM(left.shape, BF16),
            pltpu.SemaphoreType.DMA((4,)),
        ],
        HBM,
    )
    return wave[None], res[None]


def solution(mesh):
    in_specs = (
        P("freq", None, "tcol", None),
        P("freq", None, "tcol", None),
        P("freq", None, "tcol", None),
        P("freq", None, None),
        P("freq"),
    )
    out_specs = (P("freq", None, "tcol", None), P("freq", None, "tcol", None))
    return jax.shard_map(body, mesh=mesh, in_specs=in_specs, out_specs=out_specs, check_vma=False)
```

profile of v0, /device:TPU:0, one launch (start us, length us, event | category | flops | bytes accessed | tf_op | source)
XLA Modules:
  0.0 71.1 jit_solution(11748397927613758583)
XLA Ops:
  0.6 1.8 %shard_map.68 = (bf16[288,256]{1,0:T(8,128)(2,1)S(1)}, bf16[384,256]{1,0:T(8,128)(2,1)S(1)}, bf16[320,256]{1,0:T(8,128)(2,1)S(1)}, bf16[32,256]{1,0:T(8,128)(2,1...) custom-call(s32[1]{0:T(128)} %bitcast.3.here_ref, s32[1]{0:T(128)} %bitcast.4.mine_ref, s32[8,8]{1,0:T(8,128)} %bitcast.14, ...), custom_call_target="tpu_custom_call" | custom-call | tf_op jit(solution)/shard_map/pallas_call | solution.py:666
  2.4 3.1 %collective-permute-start = (bf16[384,256]{1,0:T(8,128)(2,1)S(1)}, bf16[384,256]{1,0:T(8,128)(2,1)S(1)}, u32[]{:S(2)}, u32[]{:S(2)}) collective-permute-start(bf16[384,256]{1,0:T(8,128)(2,1)S(1)} %get-tuple-element.22), channel_id=1, source_target_pairs={{0,2},{1,3},{2,4},{3,5},{4,6},{5,7},{6,0},{7,1},{8,10},{9,11},{10,... | collective-permute-start | bytes 589832 | tf_op jit(solution)/shard_map/ppermute | solution.py:703
  6.0 1.6 %collective-permute-start.7 = (bf16[256,256]{1,0:T(8,128)(2,1)S(1)}, bf16[256,256]{1,0:T(8,128)(2,1)S(1)}, u32[]{:S(2)}, u32[]{:S(2)}) collective-permute-start(bf16[256,256]{1,0:T(8,128)(2,1)S(1)} %shard_map.69.refs_8_), channel_id=1, source_target_pairs={{0,2},{1,3},{2,4},{3,5},{4,6},{5,7},{6,0},{7,1},{8,10},{9,11},{10,... | collective-permute-start | bytes 393224 | tf_op jit(solution)/shard_map/ppermute | solution.py:703
  7.6 5.7 %collective-permute-done.refs_1_ = bf16[384,256]{1,0:T(8,128)(2,1)S(1)} collective-permute-done((bf16[384,256]{1,0:T(8,128)(2,1)S(1)}, bf16[384,256]{1,0:T(8,128)(2,1)S(1)}, u32[]{:S(2)}, u32[]{:S(2)}) %collective-permute-start) | collective-permute-done | bytes 196640 | tf_op jit(solution)/shard_map/ppermute | solution.py:703
  13.3 2.0 %collective-permute-start.1 = (bf16[320,256]{1,0:T(8,128)(2,1)S(1)}, bf16[320,256]{1,0:T(8,128)(2,1)S(1)}, u32[]{:S(2)}, u32[]{:S(2)}) collective-permute-start(bf16[320,256]{1,0:T(8,128)(2,1)S(1)} %get-tuple-element.24), channel_id=1, source_target_pairs={{0,6},{1,7},{2,0},{3,1},{4,2},{5,3},{6,4},{7,5},{8,14},{9,15},{10,... | collective-permute-start | bytes 491528 | tf_op jit(solution)/shard_map/ppermute | solution.py:703
  15.3 0.8 %collective-permute-done.7.refs_9_ = bf16[256,256]{1,0:T(8,128)(2,1)S(1)} collective-permute-done((bf16[256,256]{1,0:T(8,128)(2,1)S(1)}, bf16[256,256]{1,0:T(8,128)(2,1)S(1)}, u32[]{:S(2)}, u32[]{:S(2)}) %collective-permute-start.7) | collective-permute-done | bytes 131104 | tf_op jit(solution)/shard_map/ppermute | solution.py:703
  16.1 0.9 %collective-permute-start.8 = (bf16[256,256]{1,0:T(8,128)(2,1)S(1)}, bf16[256,256]{1,0:T(8,128)(2,1)S(1)}, u32[]{:S(2)}, u32[]{:S(2)}) collective-permute-start(bf16[256,256]{1,0:T(8,128)(2,1)S(1)} %shard_map.69.refs_8_), channel_id=1, source_target_pairs={{0,6},{1,7},{2,0},{3,1},{4,2},{5,3},{6,4},{7,5},{8,14},{9,15},{10,... | collective-permute-start | bytes 393224 | tf_op jit(solution)/shard_map/ppermute | solution.py:703
  17.0 3.3 %collective-permute-done.1.refs_2_ = bf16[320,256]{1,0:T(8,128)(2,1)S(1)} collective-permute-done((bf16[320,256]{1,0:T(8,128)(2,1)S(1)}, bf16[320,256]{1,0:T(8,128)(2,1)S(1)}, u32[]{:S(2)}, u32[]{:S(2)}) %collective-permute-start.1) | collective-permute-done | bytes 163872 | tf_op jit(solution)/shard_map/ppermute | solution.py:703
  20.4 1.5 %collective-permute-start.3 = (bf16[288,256]{1,0:T(8,128)(2,1)S(1)}, bf16[288,256]{1,0:T(8,128)(2,1)S(1)}, u32[]{:S(2)}, u32[]{:S(2)}) collective-permute-start(bf16[288,256]{1,0:T(8,128)(2,1)S(1)} %get-tuple-element.21.refs_0_), channel_id=1, source_target_pairs={{0,1},{1,0},{2,3},{3,2},{4,5},{5,4},{6,7},{7,6},{8,9},{9,8},{10,11... | collective-permute-start | bytes 442376 | tf_op jit(solution)/shard_map/ppermute | solution.py:703
  22.5 1.5 %collective-permute-start.11 = (bf16[256,256]{1,0:T(8,128)(2,1)S(1)}, bf16[256,256]{1,0:T(8,128)(2,1)S(1)}, u32[]{:S(2)}, u32[]{:S(2)}) collective-permute-start(bf16[256,256]{1,0:T(8,128)(2,1)S(1)} %collective-permute-done.7.refs_9_), channel_id=1, source_target_pairs={{0,1},{1,0},{2,3},{3,2},{4,5},{5,4},{6,7},{7,6},{8,9},{9,8},{10,11... | collective-permute-start | bytes 393224 | tf_op jit(solution)/shard_map/ppermute | solution.py:703
  24.0 0.9 %collective-permute-start.9 = (bf16[256,256]{1,0:T(8,128)(2,1)S(1)}, bf16[256,256]{1,0:T(8,128)(2,1)S(1)}, u32[]{:S(2)}, u32[]{:S(2)}) collective-permute-start(bf16[256,256]{1,0:T(8,128)(2,1)S(1)} %collective-permute-done.7.refs_9_), channel_id=1, source_target_pairs={{0,2},{1,3},{2,4},{3,5},{4,6},{5,7},{6,0},{7,1},{8,10},{9,11},{10,... | collective-permute-start | bytes 393224 | tf_op jit(solution)/shard_map/ppermute | solution.py:703
  24.9 5.1 %collective-permute-done.10.refs_12_ = bf16[256,256]{1,0:T(8,128)(2,1)S(1)} collective-permute-done((bf16[256,256]{1,0:T(8,128)(2,1)S(1)}, bf16[256,256]{1,0:T(8,128)(2,1)S(1)}, u32[]{:S(2)}, u32[]{:S(2)}) %collective-permute-start.10) | collective-permute-done | bytes 131104 | tf_op jit(solution)/shard_map/ppermute | solution.py:703
  30.0 1.5 %collective-permute-start.4 = (bf16[320,256]{1,0:T(8,128)(2,1)S(1)}, bf16[320,256]{1,0:T(8,128)(2,1)S(1)}, u32[]{:S(2)}, u32[]{:S(2)}) collective-permute-start(bf16[320,256]{1,0:T(8,128)(2,1)S(1)} %slice.8), channel_id=1, source_target_pairs={{0,1},{1,0},{2,3},{3,2},{4,5},{5,4},{6,7},{7,6},{8,9},{9,8},{10,11... | collective-permute-start | bytes 491528 | tf_op jit(solution)/shard_map/ppermute | solution.py:703
  32.0 1.5 %collective-permute-start.6 = (bf16[320,256]{1,0:T(8,128)(2,1)S(1)}, bf16[320,256]{1,0:T(8,128)(2,1)S(1)}, u32[]{:S(2)}, u32[]{:S(2)}) collective-permute-start(bf16[320,256]{1,0:T(8,128)(2,1)S(1)} %collective-permute-done.2.refs_3_), channel_id=1, source_target_pairs={{0,1},{1,0},{2,3},{3,2},{4,5},{5,4},{6,7},{7,6},{8,9},{9,8},{10,11... | collective-permute-start | bytes 491528 | tf_op jit(solution)/shard_map/ppermute | solution.py:703
  34.3 1.3 %collective-permute-start.13 = (bf16[256,256]{1,0:T(8,128)(2,1)S(1)}, bf16[256,256]{1,0:T(8,128)(2,1)S(1)}, u32[]{:S(2)}, u32[]{:S(2)}) collective-permute-start(bf16[256,256]{1,0:T(8,128)(2,1)S(1)} %collective-permute-done.9.refs_11_), channel_id=1, source_target_pairs={{0,1},{1,0},{2,3},{3,2},{4,5},{5,4},{6,7},{7,6},{8,9},{9,8},{10,11... | collective-permute-start | bytes 393224 | tf_op jit(solution)/shard_map/ppermute | solution.py:703
  36.2 0.8 %collective-permute-done.4.refs_5_ = bf16[320,256]{1,0:T(8,128)(2,1)S(1)} collective-permute-done((bf16[320,256]{1,0:T(8,128)(2,1)S(1)}, bf16[320,256]{1,0:T(8,128)(2,1)S(1)}, u32[]{:S(2)}, u32[]{:S(2)}) %collective-permute-start.4) | collective-permute-done | bytes 163872 | tf_op jit(solution)/shard_map/ppermute | solution.py:703
  37.0 7.3 %collective-permute-done.12.refs_14_ = bf16[256,256]{1,0:T(8,128)(2,1)S(1)} collective-permute-done((bf16[256,256]{1,0:T(8,128)(2,1)S(1)}, bf16[256,256]{1,0:T(8,128)(2,1)S(1)}, u32[]{:S(2)}, u32[]{:S(2)}) %collective-permute-start.12) | collective-permute-done | bytes 131104 | tf_op jit(solution)/shard_map/ppermute | solution.py:703
  44.3 1.4 %collective-permute-done.13.refs_15_ = bf16[256,256]{1,0:T(8,128)(2,1)S(1)} collective-permute-done((bf16[256,256]{1,0:T(8,128)(2,1)S(1)}, bf16[256,256]{1,0:T(8,128)(2,1)S(1)}, u32[]{:S(2)}, u32[]{:S(2)}) %collective-permute-start.13) | collective-permute-done | bytes 131104 | tf_op jit(solution)/shard_map/ppermute | solution.py:703
  45.7 4.8 %shard_map.70 = (f32[3,8,32,256]{3,2,1,0:T(8,128)S(1)}, f32[3,8,32,256]{3,2,1,0:T(8,128)S(1)}, f32[16,128]{1,0:T(8,128)S(1)}) custom-call(s32[1]{0:T(128)} %bitcast.3.here_ref, s32[1]{0:T(128)S(6)} %copy.7.freq_ref, bf16[288,256]{1,0:T(8,128)(2,1)S(1)} %get-tuple-element.21.refs_0_, bf16[384,256]{1,0:T(8,128)(2,1)S(1)} %collective-permute-done.refs_1_, ...), custom_call_target="tpu_custom_call" | custom-call | tf_op jit(solution)/shard_map/pallas_call | solution.py:666
  50.6 1.6 %collective-permute-start.15 = (f32[16,128]{1,0:T(8,128)S(1)}, f32[16,128]{1,0:T(8,128)S(1)}, u32[]{:S(2)}, u32[]{:S(2)}) collective-permute-start(f32[16,128]{1,0:T(8,128)S(1)} %get-tuple-element.31.refs_0_), channel_id=1, source_target_pairs={{0,16},{8,24},{16,0},{24,8},{1,17},{9,25},{17,1},{25,9},{2,18},{10... | collective-permute-start | bytes 24584 | tf_op jit(solution)/shard_map/ppermute | solution.py:735
  52.4 1.3 %collective-permute-done.16.refs_3_ = f32[16,128]{1,0:T(8,128)S(1)} collective-permute-done((f32[16,128]{1,0:T(8,128)S(1)}, f32[16,128]{1,0:T(8,128)S(1)}, u32[]{:S(2)}, u32[]{:S(2)}) %collective-permute-start.16) | collective-permute-done | bytes 8224 | tf_op jit(solution)/shard_map/ppermute | solution.py:735
  54.3 1.3 %shard_map.71 = (bf16[8,64,256]{2,1,0:T(8,128)(2,1)S(1)}, bf16[2,512,128]{2,1,0:T(8,128)(2,1)S(1)}, bf16[2,512,256]{2,1,0:T(8,128)(2,1)S(1)}, bf16[2,512,256]{2,1,0:T(8,128)(2,1)S(1)}) custom-call(bf16[2,512,128]{2,1,0:T(8,128)(2,1)} %bitcast.13, bf16[2,512,256]{2,1,0:T(8,128)(2,1)} %bitcast.9, bf16[2,512,256]{2,1,0:T(8,128)(2,1)} %bitcast.11, ...), custom_call_target="tpu_custom_call" | custom-call | tf_op jit(solution)/shard_map/pallas_call | solution.py:666
  55.6 14.2 %all_to_all.5.recv_ref = bf16[8,64,256]{2,1,0:T(8,128)(2,1)S(1)} all-to-all(bf16[8,64,256]{2,1,0:T(8,128)(2,1)S(1)} %get-tuple-element.34), channel_id=1, replica_groups=mesh['freq'=4,'tcol'=8] {'tcol'}, dimensions={0} | all-to-all | bytes 524288 | tf_op jit(solution)/shard_map/all_to_all | solution.py:747
  69.8 1.3 %shard_map.72 = (f32[2,512,128]{2,1,0:T(8,128)}, f32[2,512,128]{2,1,0:T(8,128)}) custom-call(bf16[8,64,256]{2,1,0:T(8,128)(2,1)S(1)} %all_to_all.5.recv_ref, bf16[2,512,128]{2,1,0:T(8,128)(2,1)S(1)} %get-tuple-element.35.data_ref, bf16[2,512,256]{2,1,0:T(8,128)(2,1)S(1)} %get-tuple-element.36.left_ref, bf16[2,512,256]{2,1,0:T(8,128)(2,1)S(1)} %get-tuple-element.37.right_ref), custom_call_target="tpu_custom_call" | custom-call | tf_op jit(solution)/shard_map/pallas_call | solution.py:666
  (18 shorter events, 3.4 us)
Async XLA Ops:
  2.4 10.9 %collective-permute-start = (bf16[384,256]{1,0:T(8,128)(2,1)S(1)}, bf16[384,256]{1,0:T(8,128)(2,1)S(1)}, u32[]{:S(2)}, u32[]{:S(2)}) collective-permute-start(bf16[384,256]{1,0:T(8,128)(2,1)S(1)} %get-tuple-element.22), channel_id=1, source_target_pairs={{0,2},{1,3},{2,4},{3,5},{4,6},{5,7},{6,0},{7,1},{8,10},{9,11},{10,... | collective-permute-start | bytes 589832 | tf_op jit(solution)/shard_map/ppermute | solution.py:703
  6.0 10.1 %collective-permute-start.7 = (bf16[256,256]{1,0:T(8,128)(2,1)S(1)}, bf16[256,256]{1,0:T(8,128)(2,1)S(1)}, u32[]{:S(2)}, u32[]{:S(2)}) collective-permute-start(bf16[256,256]{1,0:T(8,128)(2,1)S(1)} %shard_map.69.refs_8_), channel_id=1, source_target_pairs={{0,2},{1,3},{2,4},{3,5},{4,6},{5,7},{6,0},{7,1},{8,10},{9,11},{10,... | collective-permute-start | bytes 393224 | tf_op jit(solution)/shard_map/ppermute | solution.py:703
  13.3 7.0 %collective-permute-start.1 = (bf16[320,256]{1,0:T(8,128)(2,1)S(1)}, bf16[320,256]{1,0:T(8,128)(2,1)S(1)}, u32[]{:S(2)}, u32[]{:S(2)}) collective-permute-start(bf16[320,256]{1,0:T(8,128)(2,1)S(1)} %get-tuple-element.24), channel_id=1, source_target_pairs={{0,6},{1,7},{2,0},{3,1},{4,2},{5,3},{6,4},{7,5},{8,14},{9,15},{10,... | collective-permute-start | bytes 491528 | tf_op jit(solution)/shard_map/ppermute | solution.py:703
  16.1 7.9 %collective-permute-start.8 = (bf16[256,256]{1,0:T(8,128)(2,1)S(1)}, bf16[256,256]{1,0:T(8,128)(2,1)S(1)}, u32[]{:S(2)}, u32[]{:S(2)}) collective-permute-start(bf16[256,256]{1,0:T(8,128)(2,1)S(1)} %shard_map.69.refs_8_), channel_id=1, source_target_pairs={{0,6},{1,7},{2,0},{3,1},{4,2},{5,3},{6,4},{7,5},{8,14},{9,15},{10,... | collective-permute-start | bytes 393224 | tf_op jit(solution)/shard_map/ppermute | solution.py:703
  20.3 11.7 %collective-permute-start.2 = (bf16[320,256]{1,0:T(8,128)(2,1)S(1)}, bf16[320,256]{1,0:T(8,128)(2,1)S(1)}, u32[]{:S(2)}, u32[]{:S(2)}) collective-permute-start(bf16[320,256]{1,0:T(8,128)(2,1)S(1)} %slice.6), channel_id=1, source_target_pairs={{0,2},{1,3},{2,4},{3,5},{4,6},{5,7},{6,0},{7,1},{8,10},{9,11},{10,... | collective-permute-start | bytes 491528 | tf_op jit(solution)/shard_map/ppermute | solution.py:703
  20.4 11.0 %collective-permute-start.3 = (bf16[288,256]{1,0:T(8,128)(2,1)S(1)}, bf16[288,256]{1,0:T(8,128)(2,1)S(1)}, u32[]{:S(2)}, u32[]{:S(2)}) collective-permute-start(bf16[288,256]{1,0:T(8,128)(2,1)S(1)} %get-tuple-element.21.refs_0_), channel_id=1, source_target_pairs={{0,1},{1,0},{2,3},{3,2},{4,5},{5,4},{6,7},{7,6},{8,9},{9,8},{10,11... | collective-permute-start | bytes 442376 | tf_op jit(solution)/shard_map/ppermute | solution.py:703
  22.0 8.0 %collective-permute-start.10 = (bf16[256,256]{1,0:T(8,128)(2,1)S(1)}, bf16[256,256]{1,0:T(8,128)(2,1)S(1)}, u32[]{:S(2)}, u32[]{:S(2)}) collective-permute-start(bf16[256,256]{1,0:T(8,128)(2,1)S(1)} %shard_map.69.refs_8_), channel_id=1, source_target_pairs={{0,1},{1,0},{2,3},{3,2},{4,5},{5,4},{6,7},{7,6},{8,9},{9,8},{10,11... | collective-permute-start | bytes 393224 | tf_op jit(solution)/shard_map/ppermute | solution.py:703
  22.5 11.0 %collective-permute-start.11 = (bf16[256,256]{1,0:T(8,128)(2,1)S(1)}, bf16[256,256]{1,0:T(8,128)(2,1)S(1)}, u32[]{:S(2)}, u32[]{:S(2)}) collective-permute-start(bf16[256,256]{1,0:T(8,128)(2,1)S(1)} %collective-permute-done.7.refs_9_), channel_id=1, source_target_pairs={{0,1},{1,0},{2,3},{3,2},{4,5},{5,4},{6,7},{7,6},{8,9},{9,8},{10,11... | collective-permute-start | bytes 393224 | tf_op jit(solution)/shard_map/ppermute | solution.py:703
  24.0 10.3 %collective-permute-start.9 = (bf16[256,256]{1,0:T(8,128)(2,1)S(1)}, bf16[256,256]{1,0:T(8,128)(2,1)S(1)}, u32[]{:S(2)}, u32[]{:S(2)}) collective-permute-start(bf16[256,256]{1,0:T(8,128)(2,1)S(1)} %collective-permute-done.7.refs_9_), channel_id=1, source_target_pairs={{0,2},{1,3},{2,4},{3,5},{4,6},{5,7},{6,0},{7,1},{8,10},{9,11},{10,... | collective-permute-start | bytes 393224 | tf_op jit(solution)/shard_map/ppermute | solution.py:703
  30.0 7.1 %collective-permute-start.4 = (bf16[320,256]{1,0:T(8,128)(2,1)S(1)}, bf16[320,256]{1,0:T(8,128)(2,1)S(1)}, u32[]{:S(2)}, u32[]{:S(2)}) collective-permute-start(bf16[320,256]{1,0:T(8,128)(2,1)S(1)} %slice.8), channel_id=1, source_target_pairs={{0,1},{1,0},{2,3},{3,2},{4,5},{5,4},{6,7},{7,6},{8,9},{9,8},{10,11... | collective-permute-start | bytes 491528 | tf_op jit(solution)/shard_map/ppermute | solution.py:703
  31.5 14.3 %collective-permute-start.5 = (bf16[320,256]{1,0:T(8,128)(2,1)S(1)}, bf16[320,256]{1,0:T(8,128)(2,1)S(1)}, u32[]{:S(2)}, u32[]{:S(2)}) collective-permute-start(bf16[320,256]{1,0:T(8,128)(2,1)S(1)} %collective-permute-done.1.refs_2_), channel_id=1, source_target_pairs={{0,1},{1,0},{2,3},{3,2},{4,5},{5,4},{6,7},{7,6},{8,9},{9,8},{10,11... | collective-permute-start | bytes 491528 | tf_op jit(solution)/shard_map/ppermute | solution.py:703
  32.0 13.7 %collective-permute-start.6 = (bf16[320,256]{1,0:T(8,128)(2,1)S(1)}, bf16[320,256]{1,0:T(8,128)(2,1)S(1)}, u32[]{:S(2)}, u32[]{:S(2)}) collective-permute-start(bf16[320,256]{1,0:T(8,128)(2,1)S(1)} %collective-permute-done.2.refs_3_), channel_id=1, source_target_pairs={{0,1},{1,0},{2,3},{3,2},{4,5},{5,4},{6,7},{7,6},{8,9},{9,8},{10,11... | collective-permute-start | bytes 491528 | tf_op jit(solution)/shard_map/ppermute | solution.py:703
  33.5 10.8 %collective-permute-start.12 = (bf16[256,256]{1,0:T(8,128)(2,1)S(1)}, bf16[256,256]{1,0:T(8,128)(2,1)S(1)}, u32[]{:S(2)}, u32[]{:S(2)}) collective-permute-start(bf16[256,256]{1,0:T(8,128)(2,1)S(1)} %collective-permute-done.8.refs_10_), channel_id=1, source_target_pairs={{0,1},{1,0},{2,3},{3,2},{4,5},{5,4},{6,7},{7,6},{8,9},{9,8},{10,11... | collective-permute-start | bytes 393224 | tf_op jit(solution)/shard_map/ppermute | solution.py:703
  34.3 11.4 %collective-permute-start.13 = (bf16[256,256]{1,0:T(8,128)(2,1)S(1)}, bf16[256,256]{1,0:T(8,128)(2,1)S(1)}, u32[]{:S(2)}, u32[]{:S(2)}) collective-permute-start(bf16[256,256]{1,0:T(8,128)(2,1)S(1)} %collective-permute-done.9.refs_11_), channel_id=1, source_target_pairs={{0,1},{1,0},{2,3},{3,2},{4,5},{5,4},{6,7},{7,6},{8,9},{9,8},{10,11... | collective-permute-start | bytes 393224 | tf_op jit(solution)/shard_map/ppermute | solution.py:703
  50.5 3.2 %collective-permute-start.16 = (f32[16,128]{1,0:T(8,128)S(1)}, f32[16,128]{1,0:T(8,128)S(1)}, u32[]{:S(2)}, u32[]{:S(2)}) collective-permute-start(f32[16,128]{1,0:T(8,128)S(1)} %get-tuple-element.31.refs_0_), channel_id=1, source_target_pairs={{0,24},{8,16},{16,8},{24,0},{1,25},{9,17},{17,9},{25,1},{2,26},{10... | collective-permute-start | bytes 24584 | tf_op jit(solution)/shard_map/ppermute | solution.py:735
  50.6 3.7 %collective-permute-start.15 = (f32[16,128]{1,0:T(8,128)S(1)}, f32[16,128]{1,0:T(8,128)S(1)}, u32[]{:S(2)}, u32[]{:S(2)}) collective-permute-start(f32[16,128]{1,0:T(8,128)S(1)} %get-tuple-element.31.refs_0_), channel_id=1, source_target_pairs={{0,16},{8,24},{16,0},{24,8},{1,17},{9,25},{17,1},{25,9},{2,18},{10... | collective-permute-start | bytes 24584 | tf_op jit(solution)/shard_map/ppermute | solution.py:735
  52.1 2.2 %collective-permute-start.14 = (f32[16,128]{1,0:T(8,128)S(1)}, f32[16,128]{1,0:T(8,128)S(1)}, u32[]{:S(2)}, u32[]{:S(2)}) collective-permute-start(f32[16,128]{1,0:T(8,128)S(1)} %get-tuple-element.31.refs_0_), channel_id=1, source_target_pairs={{0,8},{8,0},{16,24},{24,16},{1,9},{9,1},{17,25},{25,17},{2,10},{10... | collective-permute-start | bytes 24584 | tf_op jit(solution)/shard_map/ppermute | solution.py:735
where the time goes:
time: 71.3 us; the launch traced here: 71.1 us
  waiting for transfers between devices  26.2 us (37%)
  starting transfers between devices  19.7 us (28%)
  blocking collectives  14.2 us (20%)
  Pallas kernels  9.62 us (13%)
  between operations  1.35 us (2%)
    ppermute x14, waiting for transfers between devices, hop(): return lax.ppermute(value, 'tcol', pairs)  24.3 us
    ppermute x14, starting transfers between devices, hop(): return lax.ppermute(value, 'tcol', pairs)  17.8 us
    all_to_all x1, blocking collectives, by_source(): back = lax.all_to_all(out, 'tcol', 0, 0, tiled=True)  14.2 us
    pallas_call x5, Pallas kernels, call(): pl.pallas_call(kernel, out_shape=outs, in_specs=specs, out_specs=[target]...  9.62 us
    ppermute x3, starting transfers between devices, by_source(): lax.ppermute(stats, 'freq', [(f, f ^ step) for f in range(nfreq)])  1.92 us
    ppermute x3, waiting for transfers between devices, by_source(): lax.ppermute(stats, 'freq', [(f, f ^ step) for f in range(nfreq)])  1.87 us
  transfers between devices with their start and end apart: 17, of which 9 were waited for; matrix products, arithmetic and copies ran while one was open for 0% of the time, Pallas kernels for 1%

commit v1 on v0

--- a/solution.py
+++ b/solution.py
@@ -405,7 +405,7 @@
     keep_ref, right_ref, ranks_ref, data_ref, left_ref, back_ref, sem = refs[-7:]
     half = n // 2
     direct = [0] + direct_offsets(half)
-    packets, own = refs[: half - 1], refs[half - 1]
+    packets, small, own = refs[: half - 1], refs[half - 1 : half + 1], refs[half + 1]
     pairs = [
         (left_hbm, left_ref), (data_hbm, data_ref), (ranks_hbm, ranks_ref),
         (right_hbm, right_ref),
@@ -429,21 +429,19 @@
     back_ref[0] = (first[:s] + second[s:]).astype(BF16)
     back_ref[1] = (first[s:] - second[:s]).astype(BF16)
     gram = packed_gram(real, imag)
-    for k, packet in zip(direct, packets):
-        place = 4 * q if k == 1 else 0
-        packet[place : place + width, :] = gram
+    for packet in packets:
+        packet[0:width, :] = gram
     z, x = lax.div(here, 2), lax.rem(here, 2)
     for k in range(half):
         base = 2 * lax.rem(z + k, half)
         for block, target in enumerate([base + 1 - x, base + x]):
             rows = pl.ds(pl.multiple_of(target * q, q), q)
             if k == 2:
-                out, place = packets[direct.index(1)], 2 * q * block
+                out, place = small[block], 0
             elif k == 0 and block == 1:
                 out, place = own, 0
             else:
                 out, place = packets[direct.index(k)], width + 2 * q * block
-                place += 4 * q if k == 1 else 0
             out[place : place + q, :] = back_ref[0, rows, :]
             out[place + q : place + 2 * q, :] = back_ref[1, rows, :]
     keep = lane_limits([ranks_ref[p, here] for p in range(n)], rank, width)
@@ -510,8 +508,8 @@
     order = [0] + direct_offsets(half) + [2]
     lefts = [refs[:half], refs[half:n]]
     rights = [refs[n : n + half], refs[n + half : 2 * n]]
-    own = refs[2 * n]
-    b_ref, c_ref, stats_ref, left_ref, right_ref, one_ref, two_ref = refs[2 * n + 1 :]
+    small, own = refs[2 * n : 2 * n + 2], refs[2 * n + 2]
+    b_ref, c_ref, stats_ref, left_ref, right_ref, one_ref, two_ref = refs[2 * n + 3 :]
     width = refs[0].shape[1]
     q = stats_ref.shape[0]
     here = here_ref[0]
@@ -521,14 +519,15 @@
         for other in range(2):
             ref = lefts[other][order.index(k)]
             at = pl.ds(base + (1 - x if other else x), 1)
-            top = 4 * q if k == 2 or (k == 1 and not other) else 0
-            grams = (ref[top : top + width, :], rights[other][order.index(k)][...])
+            grams = (ref[0:width, :], rights[other][order.index(k)][...])
             for packed, gram_ref in zip(grams, (left_ref, right_ref)):
                 real, imag = unpacked_gram(packed)
                 gram_ref[0, at] = real[None]
                 gram_ref[1, at] = imag[None]
-            start = (0 if k == 2 else top + width) + (0 if other else 2 * q)
-            if k == 0 and not other:
+            start = width + (0 if other else 2 * q)
+            if k == 2:
+                block = small[1 - other][...]
+            elif k == 0 and not other:
                 block = own[...]
             else:
                 block = ref[start : start + 2 * q, :]
@@ -672,15 +671,15 @@
             compiler_params=pltpu.CompilerParams(vmem_limit_bytes=room),
         )(*args)
 
-    def along(shift):
+    def along(shift, flip=0):
         return [
-            (2 * z + x, 2 * ((z + shift) % half) + x) for z in range(half) for x in range(2)
+            (2 * z + x, 2 * ((z + shift) % half) + (x ^ flip))
+            for z in range(half) for x in range(2)
         ]
 
     across = [(t, t ^ 1) for t in range(ntile)]
+    sizes = [width + 2 * q] + [width + 4 * q] * (half - 2) + [2 * q] * 3
     direct = direct_offsets(half)
-    sizes = [width + (8 if k == 1 else 4) * q for k in direct]
-    sizes = [width + 2 * q] + sizes + [2 * q]
     parts = call(
         functools.partial(start_left, rank, ntile), [SMEM] * 2 + [HBM] * 4,
         (here, mine, ranks, data, left, right),
@@ -711,17 +710,16 @@
             second, _ = lax.optimization_barrier((second, rights[-1]))
         lefts.append(hop(first, along(k)))
         rights.append(hop(second, along(k)))
-    first, _ = lax.optimization_barrier((lefts[1], lefts[-1]))
-    first = first[: width + 4 * q]
+    small = [hop(parts[half - block], along(2, block)) for block in (1, 0)]
+    first, _ = lax.optimization_barrier((lefts[1][:width], lefts[-1]))
     second, _ = lax.optimization_barrier((rights[1], rights[-1]))
     lefts.append(hop(first, along(1)))
     rights.append(hop(second, along(1)))
     other_lefts, other_rights = cross[:1], cross[1:]
     for place in range(1, half):
-        value = lefts[1][4 * q :] if place == 1 else lefts[place]
-        other_lefts.append(hop(value, across))
+        other_lefts.append(hop(lefts[place], across))
         other_rights.append(hop(rights[place], across))
-    packets = (*lefts, *other_lefts, *rights, *other_rights, parts[half - 1])
+    packets = (*lefts, *other_lefts, *rights, *other_rights, *small, parts[half + 1])
     vectors = jax.ShapeDtypeStruct((3, ntile, 2 * q, width), F32)
     grams = pltpu.VMEM((2, ntile, width, width), BF16)
     vector = pltpu.VMEM((ntile, 2 * q, width), F32)

time: 71.3 us -> 68.1 us (0.955)
  waiting for transfers between devices: 26.2 us -> 20 us
  starting transfers between devices: 19.7 us -> 22.9 us
    ppermute x14 -> x16, waiting for transfers between devices: 24.3 us -> 18.1 us  [hop(): return lax.ppermute(value, 'tcol', pairs)]
    ppermute x14 -> x16, starting transfers between devices: 17.8 us -> 21 us  [hop(): return lax.ppermute(value, 'tcol', pairs)]
  transfers between devices with their start and end apart: 17 -> 19, of which waited for: 9 -> 11; matrix products, arithmetic and copies ran while one was open for 0% -> 0% of each run, Pallas kernels for 1% -> 1%
where the time goes in v1:
time: 68.1 us; the launch traced here: 67.9 us
  starting transfers between devices  22.9 us (34%)
  waiting for transfers between devices  20 us (29%)
  blocking collectives  14 us (21%)
  Pallas kernels  9.61 us (14%)
  between operations  1.36 us (2%)
    ppermute x16, starting transfers between devices, hop(): return lax.ppermute(value, 'tcol', pairs)  21 us
    ppermute x16, waiting for transfers between devices, hop(): return lax.ppermute(value, 'tcol', pairs)  18.1 us
    all_to_all x1, blocking collectives, by_source(): back = lax.all_to_all(out, 'tcol', 0, 0, tiled=True)  14 us
    pallas_call x5, Pallas kernels, call(): pl.pallas_call(kernel, out_shape=outs, in_specs=specs, out_specs=[target]...  9.61 us
    ppermute x3, starting transfers between devices, by_source(): lax.ppermute(stats, 'freq', [(f, f ^ step) for f in range(nfreq)])  1.92 us
    ppermute x3, waiting for transfers between devices, by_source(): lax.ppermute(stats, 'freq', [(f, f ^ step) for f in range(nfreq)])  1.87 us
  transfers between devices with their start and end apart: 19, of which 11 were waited for; matrix products, arithmetic and copies ran while one was open for 0% of the time, Pallas kernels for 1%

profile of v1, /device:TPU:0, one launch (start us, length us, event | category | flops | bytes accessed | tf_op | source)
XLA Modules:
  0.0 67.9 jit_solution(7985430258329523169)
XLA Ops:
  0.6 1.8 %shard_map.68 = (bf16[288,256]{1,0:T(8,128)(2,1)S(1)}, bf16[320,256]{1,0:T(8,128)(2,1)S(1)}, bf16[320,256]{1,0:T(8,128)(2,1)S(1)}, bf16[32,256]{1,0:T(8,128)(2,1...) custom-call(s32[1]{0:T(128)} %bitcast.3.here_ref, ...), custom_call_target="tpu_custom_call" | custom-call | tf_op jit(solution)/shard_map/pallas_call | solution.py:665
  2.4 3.1 %collective-permute-start = (bf16[320,256]{1,0:T(8,128)(2,1)S(1)}, bf16[320,256]{1,0:T(8,128)(2,1)S(1)}, u32[]{:S(2)}, u32[]{:S(2)}) collective-permute-start(bf16[320,256]{1,0:T(8,128)(2,1)S(1)} %get-tuple-element.24), channel_id=1, source_target_pairs={{0,2},{1,3},{2,4},{3,5},{4,6},{5,7},{6,0},{7,1},{8,10},{9,11},{10,... | collective-permute-start | bytes 491528 | tf_op jit(solution)/shard_map/ppermute | solution.py:702
  6.0 1.6 %collective-permute-start.7 = (bf16[256,256]{1,0:T(8,128)(2,1)S(1)}, bf16[256,256]{1,0:T(8,128)(2,1)S(1)}, u32[]{:S(2)}, u32[]{:S(2)}) collective-permute-start(bf16[256,256]{1,0:T(8,128)(2,1)S(1)} %shard_map.69.refs_8_), channel_id=1, source_target_pairs={{0,2},{1,3},{2,4},{3,5},{4,6},{5,7},{6,0},{7,1},{8,10},{9,11},{10,... | collective-permute-start | bytes 393224 | tf_op jit(solution)/shard_map/ppermute | solution.py:702
  7.6 5.0 %collective-permute-done.refs_1_ = bf16[320,256]{1,0:T(8,128)(2,1)S(1)} collective-permute-done((bf16[320,256]{1,0:T(8,128)(2,1)S(1)}, bf16[320,256]{1,0:T(8,128)(2,1)S(1)}, u32[]{:S(2)}, u32[]{:S(2)}) %collective-permute-start) | collective-permute-done | bytes 163872 | tf_op jit(solution)/shard_map/ppermute | solution.py:702
  12.6 2.0 %collective-permute-start.1 = (bf16[320,256]{1,0:T(8,128)(2,1)S(1)}, bf16[320,256]{1,0:T(8,128)(2,1)S(1)}, u32[]{:S(2)}, u32[]{:S(2)}) collective-permute-start(bf16[320,256]{1,0:T(8,128)(2,1)S(1)} %get-tuple-element.26), channel_id=1, source_target_pairs={{0,6},{1,7},{2,0},{3,1},{4,2},{5,3},{6,4},{7,5},{8,14},{9,15},{10,... | collective-permute-start | bytes 491528 | tf_op jit(solution)/shard_map/ppermute | solution.py:702
  16.3 1.5 %collective-permute-start.3 = (bf16[288,256]{1,0:T(8,128)(2,1)S(1)}, bf16[288,256]{1,0:T(8,128)(2,1)S(1)}, u32[]{:S(2)}, u32[]{:S(2)}) collective-permute-start(bf16[288,256]{1,0:T(8,128)(2,1)S(1)} %get-tuple-element.23.refs_0_), channel_id=1, source_target_pairs={{0,1},{1,0},{2,3},{3,2},{4,5},{5,4},{6,7},{7,6},{8,9},{9,8},{10,11... | collective-permute-start | bytes 442376 | tf_op jit(solution)/shard_map/ppermute | solution.py:702
  18.3 1.0 %collective-permute-start.14 = (bf16[32,256]{1,0:T(8,128)(2,1)S(1)}, bf16[32,256]{1,0:T(8,128)(2,1)S(1)}, u32[]{:S(2)}, u32[]{:S(2)}) collective-permute-start(bf16[32,256]{1,0:T(8,128)(2,1)S(1)} %get-tuple-element.32), channel_id=1, source_target_pairs={{0,5},{1,4},{2,7},{3,6},{4,1},{5,0},{6,3},{7,2},{8,13},{9,12},{10,... | collective-permute-start | bytes 49160 | tf_op jit(solution)/shard_map/ppermute | solution.py:702
  19.3 1.7 %collective-permute-done.8.refs_10_ = bf16[256,256]{1,0:T(8,128)(2,1)S(1)} collective-permute-done((bf16[256,256]{1,0:T(8,128)(2,1)S(1)}, bf16[256,256]{1,0:T(8,128)(2,1)S(1)}, u32[]{:S(2)}, u32[]{:S(2)}) %collective-permute-start.8) | collective-permute-done | bytes 131104 | tf_op jit(solution)/shard_map/ppermute | solution.py:702
  21.0 1.2 %collective-permute-start.15 = (bf16[32,256]{1,0:T(8,128)(2,1)S(1)}, bf16[32,256]{1,0:T(8,128)(2,1)S(1)}, u32[]{:S(2)}, u32[]{:S(2)}) collective-permute-start(bf16[32,256]{1,0:T(8,128)(2,1)S(1)} %get-tuple-element.33), channel_id=1, source_target_pairs={{0,4},{1,5},{2,6},{3,7},{4,0},{5,1},{6,2},{7,3},{8,12},{9,13},{10,... | collective-permute-start | bytes 49160 | tf_op jit(solution)/shard_map/ppermute | solution.py:702
  22.2 1.0 %collective-permute-start.11 = (bf16[256,256]{1,0:T(8,128)(2,1)S(1)}, bf16[256,256]{1,0:T(8,128)(2,1)S(1)}, u32[]{:S(2)}, u32[]{:S(2)}) collective-permute-start(bf16[256,256]{1,0:T(8,128)(2,1)S(1)} %collective-permute-done.7.refs_9_), channel_id=1, source_target_pairs={{0,1},{1,0},{2,3},{3,2},{4,5},{5,4},{6,7},{7,6},{8,9},{9,8},{10,11... | collective-permute-start | bytes 393224 | tf_op jit(solution)/shard_map/ppermute | solution.py:702
  24.0 2.8 %collective-permute-start.9 = (bf16[256,256]{1,0:T(8,128)(2,1)S(1)}, bf16[256,256]{1,0:T(8,128)(2,1)S(1)}, u32[]{:S(2)}, u32[]{:S(2)}) collective-permute-start(bf16[256,256]{1,0:T(8,128)(2,1)S(1)} %collective-permute-done.7.refs_9_), channel_id=1, source_target_pairs={{0,2},{1,3},{2,4},{3,5},{4,6},{5,7},{6,0},{7,1},{8,10},{9,11},{10,... | collective-permute-start | bytes 393224 | tf_op jit(solution)/shard_map/ppermute | solution.py:702
  26.9 1.7 %collective-permute-start.4 = (bf16[320,256]{1,0:T(8,128)(2,1)S(1)}, bf16[320,256]{1,0:T(8,128)(2,1)S(1)}, u32[]{:S(2)}, u32[]{:S(2)}) collective-permute-start(bf16[320,256]{1,0:T(8,128)(2,1)S(1)} %collective-permute-done.refs_1_), channel_id=1, source_target_pairs={{0,1},{1,0},{2,3},{3,2},{4,5},{5,4},{6,7},{7,6},{8,9},{9,8},{10,11... | collective-permute-start | bytes 491528 | tf_op jit(solution)/shard_map/ppermute | solution.py:702
  29.0 1.7 %collective-permute-start.12 = (bf16[256,256]{1,0:T(8,128)(2,1)S(1)}, bf16[256,256]{1,0:T(8,128)(2,1)S(1)}, u32[]{:S(2)}, u32[]{:S(2)}) collective-permute-start(bf16[256,256]{1,0:T(8,128)(2,1)S(1)} %collective-permute-done.8.refs_10_), channel_id=1, source_target_pairs={{0,1},{1,0},{2,3},{3,2},{4,5},{5,4},{6,7},{7,6},{8,9},{9,8},{10,11... | collective-permute-start | bytes 393224 | tf_op jit(solution)/shard_map/ppermute | solution.py:702
  31.1 1.1 %collective-permute-start.13 = (bf16[256,256]{1,0:T(8,128)(2,1)S(1)}, bf16[256,256]{1,0:T(8,128)(2,1)S(1)}, u32[]{:S(2)}, u32[]{:S(2)}) collective-permute-start(bf16[256,256]{1,0:T(8,128)(2,1)S(1)} %collective-permute-done.9.refs_11_), channel_id=1, source_target_pairs={{0,1},{1,0},{2,3},{3,2},{4,5},{5,4},{6,7},{7,6},{8,9},{9,8},{10,11... | collective-permute-start | bytes 393224 | tf_op jit(solution)/shard_map/ppermute | solution.py:702
  32.2 1.4 %collective-permute-done.2.refs_3_ = bf16[256,256]{1,0:T(8,128)(2,1)S(1)} collective-permute-done((bf16[256,256]{1,0:T(8,128)(2,1)S(1)}, bf16[256,256]{1,0:T(8,128)(2,1)S(1)}, u32[]{:S(2)}, u32[]{:S(2)}) %collective-permute-start.2) | collective-permute-done | bytes 131104 | tf_op jit(solution)/shard_map/ppermute | solution.py:702
  34.7 5.2 %collective-permute-done.12.refs_14_ = bf16[256,256]{1,0:T(8,128)(2,1)S(1)} collective-permute-done((bf16[256,256]{1,0:T(8,128)(2,1)S(1)}, bf16[256,256]{1,0:T(8,128)(2,1)S(1)}, u32[]{:S(2)}, u32[]{:S(2)}) %collective-permute-start.12) | collective-permute-done | bytes 131104 | tf_op jit(solution)/shard_map/ppermute | solution.py:702
  39.9 1.4 %collective-permute-done.13.refs_15_ = bf16[256,256]{1,0:T(8,128)(2,1)S(1)} collective-permute-done((bf16[256,256]{1,0:T(8,128)(2,1)S(1)}, bf16[256,256]{1,0:T(8,128)(2,1)S(1)}, u32[]{:S(2)}, u32[]{:S(2)}) %collective-permute-start.13) | collective-permute-done | bytes 131104 | tf_op jit(solution)/shard_map/ppermute | solution.py:702
  41.3 1.4 %collective-permute-done.6.refs_7_ = bf16[256,256]{1,0:T(8,128)(2,1)S(1)} collective-permute-done((bf16[256,256]{1,0:T(8,128)(2,1)S(1)}, bf16[256,256]{1,0:T(8,128)(2,1)S(1)}, u32[]{:S(2)}, u32[]{:S(2)}) %collective-permute-start.6) | collective-permute-done | bytes 131104 | tf_op jit(solution)/shard_map/ppermute | solution.py:702
  42.7 4.7 %shard_map.70 = (f32[3,8,32,256]{3,2,1,0:T(8,128)S(1)}, f32[3,8,32,256]{3,2,1,0:T(8,128)S(1)}, f32[16,128]{1,0:T(8,128)S(1)}) custom-call(s32[1]{0:T(128)} %bitcast.3.here_ref, s32[1]{0:T(128)S(6)} %copy.7.freq_ref, bf16[288,256]{1,0:T(8,128)(2,1)S(1)} %get-tuple-element.23.refs_0_, bf16[320,256]{1,0:T(8,128)(2,1)S(1)} %collective-permute-done.refs_1_, ...), custom_call_target="tpu_custom_call" | custom-call | tf_op jit(solution)/shard_map/pallas_call | solution.py:665
  47.5 1.6 %collective-permute-start.17 = (f32[16,128]{1,0:T(8,128)S(1)}, f32[16,128]{1,0:T(8,128)S(1)}, u32[]{:S(2)}, u32[]{:S(2)}) collective-permute-start(f32[16,128]{1,0:T(8,128)S(1)} %get-tuple-element.35.refs_0_), channel_id=1, source_target_pairs={{0,16},{8,24},{16,0},{24,8},{1,17},{9,25},{17,1},{25,9},{2,18},{10... | collective-permute-start | bytes 24584 | tf_op jit(solution)/shard_map/ppermute | solution.py:733
  49.4 1.2 %collective-permute-done.18.refs_3_ = f32[16,128]{1,0:T(8,128)S(1)} collective-permute-done((f32[16,128]{1,0:T(8,128)S(1)}, f32[16,128]{1,0:T(8,128)S(1)}, u32[]{:S(2)}, u32[]{:S(2)}) %collective-permute-start.18) | collective-permute-done | bytes 8224 | tf_op jit(solution)/shard_map/ppermute | solution.py:733
  51.2 1.3 %shard_map.71 = (bf16[8,64,256]{2,1,0:T(8,128)(2,1)S(1)}, bf16[2,512,128]{2,1,0:T(8,128)(2,1)S(1)}, bf16[2,512,256]{2,1,0:T(8,128)(2,1)S(1)}, bf16[2,512,256]{2,1,0:T(8,128)(2,1)S(1)}) custom-call(bf16[2,512,128]{2,1,0:T(8,128)(2,1)} %bitcast.13, bf16[2,512,256]{2,1,0:T(8,128)(2,1)} %bitcast.9, bf16[2,512,256]{2,1,0:T(8,128)(2,1)} %bitcast.11, ...), custom_call_target="tpu_custom_call" | custom-call | tf_op jit(solution)/shard_map/pallas_call | solution.py:665
  52.6 14.0 %all_to_all.5.recv_ref = bf16[8,64,256]{2,1,0:T(8,128)(2,1)S(1)} all-to-all(bf16[8,64,256]{2,1,0:T(8,128)(2,1)S(1)} %get-tuple-element.38), channel_id=1, replica_groups=mesh['freq'=4,'tcol'=8] {'tcol'}, dimensions={0} | all-to-all | bytes 524288 | tf_op jit(solution)/shard_map/all_to_all | solution.py:745
  66.6 1.3 %shard_map.72 = (f32[2,512,128]{2,1,0:T(8,128)}, f32[2,512,128]{2,1,0:T(8,128)}) custom-call(bf16[8,64,256]{2,1,0:T(8,128)(2,1)S(1)} %all_to_all.5.recv_ref, bf16[2,512,128]{2,1,0:T(8,128)(2,1)S(1)} %get-tuple-element.39.data_ref, bf16[2,512,256]{2,1,0:T(8,128)(2,1)S(1)} %get-tuple-element.40.left_ref, bf16[2,512,256]{2,1,0:T(8,128)(2,1)S(1)} %get-tuple-element.41.right_ref), custom_call_target="tpu_custom_call" | custom-call | tf_op jit(solution)/shard_map/pallas_call | solution.py:665
  (21 shorter events, 5.7 us)
Async XLA Ops:
  2.4 10.2 %collective-permute-start = (bf16[320,256]{1,0:T(8,128)(2,1)S(1)}, bf16[320,256]{1,0:T(8,128)(2,1)S(1)}, u32[]{:S(2)}, u32[]{:S(2)}) collective-permute-start(bf16[320,256]{1,0:T(8,128)(2,1)S(1)} %get-tuple-element.24), channel_id=1, source_target_pairs={{0,2},{1,3},{2,4},{3,5},{4,6},{5,7},{6,0},{7,1},{8,10},{9,11},{10,... | collective-permute-start | bytes 491528 | tf_op jit(solution)/shard_map/ppermute | solution.py:702
  6.0 9.4 %collective-permute-start.7 = (bf16[256,256]{1,0:T(8,128)(2,1)S(1)}, bf16[256,256]{1,0:T(8,128)(2,1)S(1)}, u32[]{:S(2)}, u32[]{:S(2)}) collective-permute-start(bf16[256,256]{1,0:T(8,128)(2,1)S(1)} %shard_map.69.refs_8_), channel_id=1, source_target_pairs={{0,2},{1,3},{2,4},{3,5},{4,6},{5,7},{6,0},{7,1},{8,10},{9,11},{10,... | collective-permute-start | bytes 393224 | tf_op jit(solution)/shard_map/ppermute | solution.py:702
  12.6 9.6 %collective-permute-start.1 = (bf16[320,256]{1,0:T(8,128)(2,1)S(1)}, bf16[320,256]{1,0:T(8,128)(2,1)S(1)}, u32[]{:S(2)}, u32[]{:S(2)}) collective-permute-start(bf16[320,256]{1,0:T(8,128)(2,1)S(1)} %get-tuple-element.26), channel_id=1, source_target_pairs={{0,6},{1,7},{2,0},{3,1},{4,2},{5,3},{6,4},{7,5},{8,14},{9,15},{10,... | collective-permute-start | bytes 491528 | tf_op jit(solution)/shard_map/ppermute | solution.py:702
  15.4 5.6 %collective-permute-start.8 = (bf16[256,256]{1,0:T(8,128)(2,1)S(1)}, bf16[256,256]{1,0:T(8,128)(2,1)S(1)}, u32[]{:S(2)}, u32[]{:S(2)}) collective-permute-start(bf16[256,256]{1,0:T(8,128)(2,1)S(1)} %shard_map.69.refs_8_), channel_id=1, source_target_pairs={{0,6},{1,7},{2,0},{3,1},{4,2},{5,3},{6,4},{7,5},{8,14},{9,15},{10,... | collective-permute-start | bytes 393224 | tf_op jit(solution)/shard_map/ppermute | solution.py:702
  16.3 12.3 %collective-permute-start.3 = (bf16[288,256]{1,0:T(8,128)(2,1)S(1)}, bf16[288,256]{1,0:T(8,128)(2,1)S(1)}, u32[]{:S(2)}, u32[]{:S(2)}) collective-permute-start(bf16[288,256]{1,0:T(8,128)(2,1)S(1)} %get-tuple-element.23.refs_0_), channel_id=1, source_target_pairs={{0,1},{1,0},{2,3},{3,2},{4,5},{5,4},{6,7},{7,6},{8,9},{9,8},{10,11... | collective-permute-start | bytes 442376 | tf_op jit(solution)/shard_map/ppermute | solution.py:702
  17.8 9.1 %collective-permute-start.10 = (bf16[256,256]{1,0:T(8,128)(2,1)S(1)}, bf16[256,256]{1,0:T(8,128)(2,1)S(1)}, u32[]{:S(2)}, u32[]{:S(2)}) collective-permute-start(bf16[256,256]{1,0:T(8,128)(2,1)S(1)} %shard_map.69.refs_8_), channel_id=1, source_target_pairs={{0,1},{1,0},{2,3},{3,2},{4,5},{5,4},{6,7},{7,6},{8,9},{9,8},{10,11... | collective-permute-start | bytes 393224 | tf_op jit(solution)/shard_map/ppermute | solution.py:702
  18.3 5.7 %collective-permute-start.14 = (bf16[32,256]{1,0:T(8,128)(2,1)S(1)}, bf16[32,256]{1,0:T(8,128)(2,1)S(1)}, u32[]{:S(2)}, u32[]{:S(2)}) collective-permute-start(bf16[32,256]{1,0:T(8,128)(2,1)S(1)} %get-tuple-element.32), channel_id=1, source_target_pairs={{0,5},{1,4},{2,7},{3,6},{4,1},{5,0},{6,3},{7,2},{8,13},{9,12},{10,... | collective-permute-start | bytes 49160 | tf_op jit(solution)/shard_map/ppermute | solution.py:702
  21.0 5.8 %collective-permute-start.15 = (bf16[32,256]{1,0:T(8,128)(2,1)S(1)}, bf16[32,256]{1,0:T(8,128)(2,1)S(1)}, u32[]{:S(2)}, u32[]{:S(2)}) collective-permute-start(bf16[32,256]{1,0:T(8,128)(2,1)S(1)} %get-tuple-element.33), channel_id=1, source_target_pairs={{0,4},{1,5},{2,6},{3,7},{4,0},{5,1},{6,2},{7,3},{8,12},{9,13},{10,... | collective-permute-start | bytes 49160 | tf_op jit(solution)/shard_map/ppermute | solution.py:702
  22.2 6.7 %collective-permute-start.11 = (bf16[256,256]{1,0:T(8,128)(2,1)S(1)}, bf16[256,256]{1,0:T(8,128)(2,1)S(1)}, u32[]{:S(2)}, u32[]{:S(2)}) collective-permute-start(bf16[256,256]{1,0:T(8,128)(2,1)S(1)} %collective-permute-done.7.refs_9_), channel_id=1, source_target_pairs={{0,1},{1,0},{2,3},{3,2},{4,5},{5,4},{6,7},{7,6},{8,9},{9,8},{10,11... | collective-permute-start | bytes 393224 | tf_op jit(solution)/shard_map/ppermute | solution.py:702
  24.0 7.1 %collective-permute-start.9 = (bf16[256,256]{1,0:T(8,128)(2,1)S(1)}, bf16[256,256]{1,0:T(8,128)(2,1)S(1)}, u32[]{:S(2)}, u32[]{:S(2)}) collective-permute-start(bf16[256,256]{1,0:T(8,128)(2,1)S(1)} %collective-permute-done.7.refs_9_), channel_id=1, source_target_pairs={{0,2},{1,3},{2,4},{3,5},{4,6},{5,7},{6,0},{7,1},{8,10},{9,11},{10,... | collective-permute-start | bytes 393224 | tf_op jit(solution)/shard_map/ppermute | solution.py:702
  26.8 6.8 %collective-permute-start.2 = (bf16[256,256]{1,0:T(8,128)(2,1)S(1)}, bf16[256,256]{1,0:T(8,128)(2,1)S(1)}, u32[]{:S(2)}, u32[]{:S(2)}) collective-permute-start(bf16[256,256]{1,0:T(8,128)(2,1)S(1)} %slice.4), channel_id=1, source_target_pairs={{0,2},{1,3},{2,4},{3,5},{4,6},{5,7},{6,0},{7,1},{8,10},{9,11},{10,... | collective-permute-start | bytes 393224 | tf_op jit(solution)/shard_map/ppermute | solution.py:702
  26.9 7.8 %collective-permute-start.4 = (bf16[320,256]{1,0:T(8,128)(2,1)S(1)}, bf16[320,256]{1,0:T(8,128)(2,1)S(1)}, u32[]{:S(2)}, u32[]{:S(2)}) collective-permute-start(bf16[320,256]{1,0:T(8,128)(2,1)S(1)} %collective-permute-done.refs_1_), channel_id=1, source_target_pairs={{0,1},{1,0},{2,3},{3,2},{4,5},{5,4},{6,7},{7,6},{8,9},{9,8},{10,11... | collective-permute-start | bytes 491528 | tf_op jit(solution)/shard_map/ppermute | solution.py:702
  28.6 11.2 %collective-permute-start.5 = (bf16[320,256]{1,0:T(8,128)(2,1)S(1)}, bf16[320,256]{1,0:T(8,128)(2,1)S(1)}, u32[]{:S(2)}, u32[]{:S(2)}) collective-permute-start(bf16[320,256]{1,0:T(8,128)(2,1)S(1)} %collective-permute-done.1.refs_2_), channel_id=1, source_target_pairs={{0,1},{1,0},{2,3},{3,2},{4,5},{5,4},{6,7},{7,6},{8,9},{9,8},{10,11... | collective-permute-start | bytes 491528 | tf_op jit(solution)/shard_map/ppermute | solution.py:702
  29.0 10.9 %collective-permute-start.12 = (bf16[256,256]{1,0:T(8,128)(2,1)S(1)}, bf16[256,256]{1,0:T(8,128)(2,1)S(1)}, u32[]{:S(2)}, u32[]{:S(2)}) collective-permute-start(bf16[256,256]{1,0:T(8,128)(2,1)S(1)} %collective-permute-done.8.refs_10_), channel_id=1, source_target_pairs={{0,1},{1,0},{2,3},{3,2},{4,5},{5,4},{6,7},{7,6},{8,9},{9,8},{10,11... | collective-permute-start | bytes 393224 | tf_op jit(solution)/shard_map/ppermute | solution.py:702
  31.1 10.2 %collective-permute-start.13 = (bf16[256,256]{1,0:T(8,128)(2,1)S(1)}, bf16[256,256]{1,0:T(8,128)(2,1)S(1)}, u32[]{:S(2)}, u32[]{:S(2)}) collective-permute-start(bf16[256,256]{1,0:T(8,128)(2,1)S(1)} %collective-permute-done.9.refs_11_), channel_id=1, source_target_pairs={{0,1},{1,0},{2,3},{3,2},{4,5},{5,4},{6,7},{7,6},{8,9},{9,8},{10,11... | collective-permute-start | bytes 393224 | tf_op jit(solution)/shard_map/ppermute | solution.py:702
  33.6 9.1 %collective-permute-start.6 = (bf16[256,256]{1,0:T(8,128)(2,1)S(1)}, bf16[256,256]{1,0:T(8,128)(2,1)S(1)}, u32[]{:S(2)}, u32[]{:S(2)}) collective-permute-start(bf16[256,256]{1,0:T(8,128)(2,1)S(1)} %collective-permute-done.2.refs_3_), channel_id=1, source_target_pairs={{0,1},{1,0},{2,3},{3,2},{4,5},{5,4},{6,7},{7,6},{8,9},{9,8},{10,11... | collective-permute-start | bytes 393224 | tf_op jit(solution)/shard_map/ppermute | solution.py:702
  47.5 3.2 %collective-permute-start.18 = (f32[16,128]{1,0:T(8,128)S(1)}, f32[16,128]{1,0:T(8,128)S(1)}, u32[]{:S(2)}, u32[]{:S(2)}) collective-permute-start(f32[16,128]{1,0:T(8,128)S(1)} %get-tuple-element.35.refs_0_), channel_id=1, source_target_pairs={{0,24},{8,16},{16,8},{24,0},{1,25},{9,17},{17,9},{25,1},{2,26},{10... | collective-permute-start | bytes 24584 | tf_op jit(solution)/shard_map/ppermute | solution.py:733
  47.5 3.7 %collective-permute-start.17 = (f32[16,128]{1,0:T(8,128)S(1)}, f32[16,128]{1,0:T(8,128)S(1)}, u32[]{:S(2)}, u32[]{:S(2)}) collective-permute-start(f32[16,128]{1,0:T(8,128)S(1)} %get-tuple-element.35.refs_0_), channel_id=1, source_target_pairs={{0,16},{8,24},{16,0},{24,8},{1,17},{9,25},{17,1},{25,9},{2,18},{10... | collective-permute-start | bytes 24584 | tf_op jit(solution)/shard_map/ppermute | solution.py:733
  49.1 2.1 %collective-permute-start.16 = (f32[16,128]{1,0:T(8,128)S(1)}, f32[16,128]{1,0:T(8,128)S(1)}, u32[]{:S(2)}, u32[]{:S(2)}) collective-permute-start(f32[16,128]{1,0:T(8,128)S(1)} %get-tuple-element.35.refs_0_), channel_id=1, source_target_pairs={{0,8},{8,0},{16,24},{24,16},{1,9},{9,1},{17,25},{25,17},{2,10},{10... | collective-permute-start | bytes 24584 | tf_op jit(solution)/shard_map/ppermute | solution.py:733

commit v2 on v1

--- a/solution.py
+++ b/solution.py
@@ -707,14 +707,11 @@
         first, second = parts[1 + place], gram
         if place:
             first, _ = lax.optimization_barrier((first, lefts[-1]))
-            second, _ = lax.optimization_barrier((second, rights[-1]))
         lefts.append(hop(first, along(k)))
         rights.append(hop(second, along(k)))
     small = [hop(parts[half - block], along(2, block)) for block in (1, 0)]
-    first, _ = lax.optimization_barrier((lefts[1][:width], lefts[-1]))
-    second, _ = lax.optimization_barrier((rights[1], rights[-1]))
-    lefts.append(hop(first, along(1)))
-    rights.append(hop(second, along(1)))
+    lefts.append(hop(lefts[1][:width], along(1)))
+    rights.append(hop(rights[1], along(1)))
     other_lefts, other_rights = cross[:1], cross[1:]
     for place in range(1, half):
         other_lefts.append(hop(lefts[place], across))

time: 68.1 us -> 67 us (0.984)
  blocking collectives: 14 us -> 12.4 us
  starting transfers between devices: 22.9 us -> 23.7 us
    all_to_all x1, blocking collectives: 14 us -> 12.4 us  [by_source(): back = lax.all_to_all(out, 'tcol', 0, 0, tiled=True)]
    ppermute x16, starting transfers between devices: 21 us -> 21.7 us  [hop(): return lax.ppermute(value, 'tcol', pairs)]
  transfers between devices with their start and end apart: 19 -> 19, of which waited for: 11 -> 10; matrix products, arithmetic and copies ran while one was open for 0% -> 0% of each run, Pallas kernels for 1% -> 1%
where the time goes in v2:
time: 67 us; the launch traced here: 66.8 us
  starting transfers between devices  23.7 us (35%)
  waiting for transfers between devices  19.7 us (29%)
  blocking collectives  12.4 us (19%)
  Pallas kernels  9.61 us (14%)
  between operations  1.36 us (2%)
    ppermute x16, starting transfers between devices, hop(): return lax.ppermute(value, 'tcol', pairs)  21.7 us
    ppermute x16, waiting for transfers between devices, hop(): return lax.ppermute(value, 'tcol', pairs)  17.8 us
    all_to_all x1, blocking collectives, by_source(): back = lax.all_to_all(out, 'tcol', 0, 0, tiled=True)  12.4 us
    pallas_call x5, Pallas kernels, call(): pl.pallas_call(kernel, out_shape=outs, in_specs=specs, out_specs=[target]...  9.61 us
    ppermute x3, starting transfers between devices, by_source(): lax.ppermute(stats, 'freq', [(f, f ^ step) for f in range(nfreq)])  1.92 us
    ppermute x3, waiting for transfers between devices, by_source(): lax.ppermute(stats, 'freq', [(f, f ^ step) for f in range(nfreq)])  1.87 us
  transfers between devices with their start and end apart: 19, of which 10 were waited for; matrix products, arithmetic and copies ran while one was open for 0% of the time, Pallas kernels for 1%

profile of v2, /device:TPU:0, one launch (start us, length us, event | category | flops | bytes accessed | tf_op | source)
XLA Modules:
  0.0 66.8 jit_solution(2396849601514527917)
XLA Ops:
  0.6 1.8 %shard_map.68 = (bf16[288,256]{1,0:T(8,128)(2,1)S(1)}, bf16[320,256]{1,0:T(8,128)(2,1)S(1)}, bf16[320,256]{1,0:T(8,128)(2,1)S(1)}, bf16[32,256]{1,0:T(8,128)(2,1...) custom-call(s32[1]{0:T(128)} %bitcast.3.here_ref, ...), custom_call_target="tpu_custom_call" | custom-call | tf_op jit(solution)/shard_map/pallas_call | solution.py:665
  2.4 3.1 %collective-permute-start = (bf16[320,256]{1,0:T(8,128)(2,1)S(1)}, bf16[320,256]{1,0:T(8,128)(2,1)S(1)}, u32[]{:S(2)}, u32[]{:S(2)}) collective-permute-start(bf16[320,256]{1,0:T(8,128)(2,1)S(1)} %get-tuple-element.21), channel_id=1, source_target_pairs={{0,2},{1,3},{2,4},{3,5},{4,6},{5,7},{6,0},{7,1},{8,10},{9,11},{10,... | collective-permute-start | bytes 491528 | tf_op jit(solution)/shard_map/ppermute | solution.py:702
  6.0 2.1 %collective-permute-start.8 = (bf16[256,256]{1,0:T(8,128)(2,1)S(1)}, bf16[256,256]{1,0:T(8,128)(2,1)S(1)}, u32[]{:S(2)}, u32[]{:S(2)}) collective-permute-start(bf16[256,256]{1,0:T(8,128)(2,1)S(1)} %shard_map.69.refs_8_), channel_id=1, source_target_pairs={{0,6},{1,7},{2,0},{3,1},{4,2},{5,3},{6,4},{7,5},{8,14},{9,15},{10,... | collective-permute-start | bytes 393224 | tf_op jit(solution)/shard_map/ppermute | solution.py:702
  8.1 1.7 %collective-permute-start.10 = (bf16[256,256]{1,0:T(8,128)(2,1)S(1)}, bf16[256,256]{1,0:T(8,128)(2,1)S(1)}, u32[]{:S(2)}, u32[]{:S(2)}) collective-permute-start(bf16[256,256]{1,0:T(8,128)(2,1)S(1)} %shard_map.69.refs_8_), channel_id=1, source_target_pairs={{0,1},{1,0},{2,3},{3,2},{4,5},{5,4},{6,7},{7,6},{8,9},{9,8},{10,11... | collective-permute-start | bytes 393224 | tf_op jit(solution)/shard_map/ppermute | solution.py:702
  9.8 2.3 %collective-permute-start.14 = (bf16[32,256]{1,0:T(8,128)(2,1)S(1)}, bf16[32,256]{1,0:T(8,128)(2,1)S(1)}, u32[]{:S(2)}, u32[]{:S(2)}) collective-permute-start(bf16[32,256]{1,0:T(8,128)(2,1)S(1)} %get-tuple-element.26), channel_id=1, source_target_pairs={{0,5},{1,4},{2,7},{3,6},{4,1},{5,0},{6,3},{7,2},{8,13},{9,12},{10,... | collective-permute-start | bytes 49160 | tf_op jit(solution)/shard_map/ppermute | solution.py:702
  12.7 3.7 %collective-permute-start.15 = (bf16[32,256]{1,0:T(8,128)(2,1)S(1)}, bf16[32,256]{1,0:T(8,128)(2,1)S(1)}, u32[]{:S(2)}, u32[]{:S(2)}) collective-permute-start(bf16[32,256]{1,0:T(8,128)(2,1)S(1)} %get-tuple-element.27), channel_id=1, source_target_pairs={{0,4},{1,5},{2,6},{3,7},{4,0},{5,1},{6,2},{7,3},{8,12},{9,13},{10,... | collective-permute-start | bytes 49160 | tf_op jit(solution)/shard_map/ppermute | solution.py:702
  16.4 2.9 %collective-permute-done.14.refs_16_ = bf16[32,256]{1,0:T(8,128)(2,1)S(1)} collective-permute-done((bf16[32,256]{1,0:T(8,128)(2,1)S(1)}, bf16[32,256]{1,0:T(8,128)(2,1)S(1)}, u32[]{:S(2)}, u32[]{:S(2)}) %collective-permute-start.14) | collective-permute-done | bytes 16416 | tf_op jit(solution)/shard_map/ppermute | solution.py:702
  19.3 1.7 %collective-permute-start.1 = (bf16[320,256]{1,0:T(8,128)(2,1)S(1)}, bf16[320,256]{1,0:T(8,128)(2,1)S(1)}, u32[]{:S(2)}, u32[]{:S(2)}) collective-permute-start(bf16[320,256]{1,0:T(8,128)(2,1)S(1)} %get-tuple-element.23), channel_id=1, source_target_pairs={{0,6},{1,7},{2,0},{3,1},{4,2},{5,3},{6,4},{7,5},{8,14},{9,15},{10,... | collective-permute-start | bytes 491528 | tf_op jit(solution)/shard_map/ppermute | solution.py:702
  21.5 1.6 %collective-permute-start.12 = (bf16[256,256]{1,0:T(8,128)(2,1)S(1)}, bf16[256,256]{1,0:T(8,128)(2,1)S(1)}, u32[]{:S(2)}, u32[]{:S(2)}) collective-permute-start(bf16[256,256]{1,0:T(8,128)(2,1)S(1)} %collective-permute-done.8.refs_10_), channel_id=1, source_target_pairs={{0,1},{1,0},{2,3},{3,2},{4,5},{5,4},{6,7},{7,6},{8,9},{9,8},{10,11... | collective-permute-start | bytes 393224 | tf_op jit(solution)/shard_map/ppermute | solution.py:702
  23.8 2.9 %collective-permute-done.3.refs_4_ = bf16[288,256]{1,0:T(8,128)(2,1)S(1)} collective-permute-done((bf16[288,256]{1,0:T(8,128)(2,1)S(1)}, bf16[288,256]{1,0:T(8,128)(2,1)S(1)}, u32[]{:S(2)}, u32[]{:S(2)}) %collective-permute-start.3) | collective-permute-done | bytes 147488 | tf_op jit(solution)/shard_map/ppermute | solution.py:702
  26.6 0.9 %collective-permute-start.4 = (bf16[320,256]{1,0:T(8,128)(2,1)S(1)}, bf16[320,256]{1,0:T(8,128)(2,1)S(1)}, u32[]{:S(2)}, u32[]{:S(2)}) collective-permute-start(bf16[320,256]{1,0:T(8,128)(2,1)S(1)} %collective-permute-done.refs_1_), channel_id=1, source_target_pairs={{0,1},{1,0},{2,3},{3,2},{4,5},{5,4},{6,7},{7,6},{8,9},{9,8},{10,11... | collective-permute-start | bytes 491528 | tf_op jit(solution)/shard_map/ppermute | solution.py:702
  28.6 0.8 %collective-permute-done.12.refs_14_ = bf16[256,256]{1,0:T(8,128)(2,1)S(1)} collective-permute-done((bf16[256,256]{1,0:T(8,128)(2,1)S(1)}, bf16[256,256]{1,0:T(8,128)(2,1)S(1)}, u32[]{:S(2)}, u32[]{:S(2)}) %collective-permute-start.12) | collective-permute-done | bytes 131104 | tf_op jit(solution)/shard_map/ppermute | solution.py:702
  29.4 0.9 %collective-permute-start.11 = (bf16[256,256]{1,0:T(8,128)(2,1)S(1)}, bf16[256,256]{1,0:T(8,128)(2,1)S(1)}, u32[]{:S(2)}, u32[]{:S(2)}) collective-permute-start(bf16[256,256]{1,0:T(8,128)(2,1)S(1)} %collective-permute-done.7.refs_9_), channel_id=1, source_target_pairs={{0,1},{1,0},{2,3},{3,2},{4,5},{5,4},{6,7},{7,6},{8,9},{9,8},{10,11... | collective-permute-start | bytes 393224 | tf_op jit(solution)/shard_map/ppermute | solution.py:702
  30.3 1.1 %collective-permute-start.13 = (bf16[256,256]{1,0:T(8,128)(2,1)S(1)}, bf16[256,256]{1,0:T(8,128)(2,1)S(1)}, u32[]{:S(2)}, u32[]{:S(2)}) collective-permute-start(bf16[256,256]{1,0:T(8,128)(2,1)S(1)} %collective-permute-done.9.refs_11_), channel_id=1, source_target_pairs={{0,1},{1,0},{2,3},{3,2},{4,5},{5,4},{6,7},{7,6},{8,9},{9,8},{10,11... | collective-permute-start | bytes 393224 | tf_op jit(solution)/shard_map/ppermute | solution.py:702
  31.4 0.9 %collective-permute-start.6 = (bf16[256,256]{1,0:T(8,128)(2,1)S(1)}, bf16[256,256]{1,0:T(8,128)(2,1)S(1)}, u32[]{:S(2)}, u32[]{:S(2)}) collective-permute-start(bf16[256,256]{1,0:T(8,128)(2,1)S(1)} %collective-permute-done.2.refs_3_), channel_id=1, source_target_pairs={{0,1},{1,0},{2,3},{3,2},{4,5},{5,4},{6,7},{7,6},{8,9},{9,8},{10,11... | collective-permute-start | bytes 393224 | tf_op jit(solution)/shard_map/ppermute | solution.py:702
  33.0 7.0 %collective-permute-done.11.refs_13_ = bf16[256,256]{1,0:T(8,128)(2,1)S(1)} collective-permute-done((bf16[256,256]{1,0:T(8,128)(2,1)S(1)}, bf16[256,256]{1,0:T(8,128)(2,1)S(1)}, u32[]{:S(2)}, u32[]{:S(2)}) %collective-permute-start.11) | collective-permute-done | bytes 131104 | tf_op jit(solution)/shard_map/ppermute | solution.py:702
  40.0 1.8 %collective-permute-done.13.refs_15_ = bf16[256,256]{1,0:T(8,128)(2,1)S(1)} collective-permute-done((bf16[256,256]{1,0:T(8,128)(2,1)S(1)}, bf16[256,256]{1,0:T(8,128)(2,1)S(1)}, u32[]{:S(2)}, u32[]{:S(2)}) %collective-permute-start.13) | collective-permute-done | bytes 131104 | tf_op jit(solution)/shard_map/ppermute | solution.py:702
  41.8 1.4 %collective-permute-done.6.refs_7_ = bf16[256,256]{1,0:T(8,128)(2,1)S(1)} collective-permute-done((bf16[256,256]{1,0:T(8,128)(2,1)S(1)}, bf16[256,256]{1,0:T(8,128)(2,1)S(1)}, u32[]{:S(2)}, u32[]{:S(2)}) %collective-permute-start.6) | collective-permute-done | bytes 131104 | tf_op jit(solution)/shard_map/ppermute | solution.py:702
  43.2 4.7 %shard_map.70 = (f32[3,8,32,256]{3,2,1,0:T(8,128)S(1)}, f32[3,8,32,256]{3,2,1,0:T(8,128)S(1)}, f32[16,128]{1,0:T(8,128)S(1)}) custom-call(s32[1]{0:T(128)} %bitcast.3.here_ref, s32[1]{0:T(128)S(6)} %copy.7.freq_ref, bf16[288,256]{1,0:T(8,128)(2,1)S(1)} %get-tuple-element.20.refs_0_, bf16[320,256]{1,0:T(8,128)(2,1)S(1)} %collective-permute-done.refs_1_, ...), custom_call_target="tpu_custom_call" | custom-call | tf_op jit(solution)/shard_map/pallas_call | solution.py:665
  48.0 1.6 %collective-permute-start.17 = (f32[16,128]{1,0:T(8,128)S(1)}, f32[16,128]{1,0:T(8,128)S(1)}, u32[]{:S(2)}, u32[]{:S(2)}) collective-permute-start(f32[16,128]{1,0:T(8,128)S(1)} %get-tuple-element.29.refs_0_), channel_id=1, source_target_pairs={{0,16},{8,24},{16,0},{24,8},{1,17},{9,25},{17,1},{25,9},{2,18},{10... | collective-permute-start | bytes 24584 | tf_op jit(solution)/shard_map/ppermute | solution.py:730
  49.9 1.2 %collective-permute-done.18.refs_3_ = f32[16,128]{1,0:T(8,128)S(1)} collective-permute-done((f32[16,128]{1,0:T(8,128)S(1)}, f32[16,128]{1,0:T(8,128)S(1)}, u32[]{:S(2)}, u32[]{:S(2)}) %collective-permute-start.18) | collective-permute-done | bytes 8224 | tf_op jit(solution)/shard_map/ppermute | solution.py:730
  51.7 1.3 %shard_map.71 = (bf16[8,64,256]{2,1,0:T(8,128)(2,1)S(1)}, bf16[2,512,128]{2,1,0:T(8,128)(2,1)S(1)}, bf16[2,512,256]{2,1,0:T(8,128)(2,1)S(1)}, bf16[2,512,256]{2,1,0:T(8,128)(2,1)S(1)}) custom-call(bf16[2,512,128]{2,1,0:T(8,128)(2,1)} %bitcast.13, bf16[2,512,256]{2,1,0:T(8,128)(2,1)} %bitcast.9, bf16[2,512,256]{2,1,0:T(8,128)(2,1)} %bitcast.11, ...), custom_call_target="tpu_custom_call" | custom-call | tf_op jit(solution)/shard_map/pallas_call | solution.py:665
  53.0 12.4 %all_to_all.5.recv_ref = bf16[8,64,256]{2,1,0:T(8,128)(2,1)S(1)} all-to-all(bf16[8,64,256]{2,1,0:T(8,128)(2,1)S(1)} %get-tuple-element.32), channel_id=1, replica_groups=mesh['freq'=4,'tcol'=8] {'tcol'}, dimensions={0} | all-to-all | bytes 524288 | tf_op jit(solution)/shard_map/all_to_all | solution.py:742
  65.5 1.3 %shard_map.72 = (f32[2,512,128]{2,1,0:T(8,128)}, f32[2,512,128]{2,1,0:T(8,128)}) custom-call(bf16[8,64,256]{2,1,0:T(8,128)(2,1)S(1)} %all_to_all.5.recv_ref, bf16[2,512,128]{2,1,0:T(8,128)(2,1)S(1)} %get-tuple-element.33.data_ref, bf16[2,512,256]{2,1,0:T(8,128)(2,1)S(1)} %get-tuple-element.34.left_ref, bf16[2,512,256]{2,1,0:T(8,128)(2,1)S(1)} %get-tuple-element.35.right_ref), custom_call_target="tpu_custom_call" | custom-call | tf_op jit(solution)/shard_map/pallas_call | solution.py:665
  (21 shorter events, 4.3 us)
Async XLA Ops:
  2.4 10.3 %collective-permute-start = (bf16[320,256]{1,0:T(8,128)(2,1)S(1)}, bf16[320,256]{1,0:T(8,128)(2,1)S(1)}, u32[]{:S(2)}, u32[]{:S(2)}) collective-permute-start(bf16[320,256]{1,0:T(8,128)(2,1)S(1)} %get-tuple-element.21), channel_id=1, source_target_pairs={{0,2},{1,3},{2,4},{3,5},{4,6},{5,7},{6,0},{7,1},{8,10},{9,11},{10,... | collective-permute-start | bytes 491528 | tf_op jit(solution)/shard_map/ppermute | solution.py:702
  6.0 15.5 %collective-permute-start.8 = (bf16[256,256]{1,0:T(8,128)(2,1)S(1)}, bf16[256,256]{1,0:T(8,128)(2,1)S(1)}, u32[]{:S(2)}, u32[]{:S(2)}) collective-permute-start(bf16[256,256]{1,0:T(8,128)(2,1)S(1)} %shard_map.69.refs_8_), channel_id=1, source_target_pairs={{0,6},{1,7},{2,0},{3,1},{4,2},{5,3},{6,4},{7,5},{8,14},{9,15},{10,... | collective-permute-start | bytes 393224 | tf_op jit(solution)/shard_map/ppermute | solution.py:702
  8.1 15.0 %collective-permute-start.7 = (bf16[256,256]{1,0:T(8,128)(2,1)S(1)}, bf16[256,256]{1,0:T(8,128)(2,1)S(1)}, u32[]{:S(2)}, u32[]{:S(2)}) collective-permute-start(bf16[256,256]{1,0:T(8,128)(2,1)S(1)} %shard_map.69.refs_8_), channel_id=1, source_target_pairs={{0,2},{1,3},{2,4},{3,5},{4,6},{5,7},{6,0},{7,1},{8,10},{9,11},{10,... | collective-permute-start | bytes 393224 | tf_op jit(solution)/shard_map/ppermute | solution.py:702
  8.1 15.4 %collective-permute-start.10 = (bf16[256,256]{1,0:T(8,128)(2,1)S(1)}, bf16[256,256]{1,0:T(8,128)(2,1)S(1)}, u32[]{:S(2)}, u32[]{:S(2)}) collective-permute-start(bf16[256,256]{1,0:T(8,128)(2,1)S(1)} %shard_map.69.refs_8_), channel_id=1, source_target_pairs={{0,1},{1,0},{2,3},{3,2},{4,5},{5,4},{6,7},{7,6},{8,9},{9,8},{10,11... | collective-permute-start | bytes 393224 | tf_op jit(solution)/shard_map/ppermute | solution.py:702
  9.8 9.5 %collective-permute-start.14 = (bf16[32,256]{1,0:T(8,128)(2,1)S(1)}, bf16[32,256]{1,0:T(8,128)(2,1)S(1)}, u32[]{:S(2)}, u32[]{:S(2)}) collective-permute-start(bf16[32,256]{1,0:T(8,128)(2,1)S(1)} %get-tuple-element.26), channel_id=1, source_target_pairs={{0,5},{1,4},{2,7},{3,6},{4,1},{5,0},{6,3},{7,2},{8,13},{9,12},{10,... | collective-permute-start | bytes 49160 | tf_op jit(solution)/shard_map/ppermute | solution.py:702
  12.7 8.3 %collective-permute-start.15 = (bf16[32,256]{1,0:T(8,128)(2,1)S(1)}, bf16[32,256]{1,0:T(8,128)(2,1)S(1)}, u32[]{:S(2)}, u32[]{:S(2)}) collective-permute-start(bf16[32,256]{1,0:T(8,128)(2,1)S(1)} %get-tuple-element.27), channel_id=1, source_target_pairs={{0,4},{1,5},{2,6},{3,7},{4,0},{5,1},{6,2},{7,3},{8,12},{9,13},{10,... | collective-permute-start | bytes 49160 | tf_op jit(solution)/shard_map/ppermute | solution.py:702
  19.3 8.7 %collective-permute-start.1 = (bf16[320,256]{1,0:T(8,128)(2,1)S(1)}, bf16[320,256]{1,0:T(8,128)(2,1)S(1)}, u32[]{:S(2)}, u32[]{:S(2)}) collective-permute-start(bf16[320,256]{1,0:T(8,128)(2,1)S(1)} %get-tuple-element.23), channel_id=1, source_target_pairs={{0,6},{1,7},{2,0},{3,1},{4,2},{5,3},{6,4},{7,5},{8,14},{9,15},{10,... | collective-permute-start | bytes 491528 | tf_op jit(solution)/shard_map/ppermute | solution.py:702
  21.0 5.6 %collective-permute-start.3 = (bf16[288,256]{1,0:T(8,128)(2,1)S(1)}, bf16[288,256]{1,0:T(8,128)(2,1)S(1)}, u32[]{:S(2)}, u32[]{:S(2)}) collective-permute-start(bf16[288,256]{1,0:T(8,128)(2,1)S(1)} %get-tuple-element.20.refs_0_), channel_id=1, source_target_pairs={{0,1},{1,0},{2,3},{3,2},{4,5},{5,4},{6,7},{7,6},{8,9},{9,8},{10,11... | collective-permute-start | bytes 442376 | tf_op jit(solution)/shard_map/ppermute | solution.py:702
  21.5 7.9 %collective-permute-start.12 = (bf16[256,256]{1,0:T(8,128)(2,1)S(1)}, bf16[256,256]{1,0:T(8,128)(2,1)S(1)}, u32[]{:S(2)}, u32[]{:S(2)}) collective-permute-start(bf16[256,256]{1,0:T(8,128)(2,1)S(1)} %collective-permute-done.8.refs_10_), channel_id=1, source_target_pairs={{0,1},{1,0},{2,3},{3,2},{4,5},{5,4},{6,7},{7,6},{8,9},{9,8},{10,11... | collective-permute-start | bytes 393224 | tf_op jit(solution)/shard_map/ppermute | solution.py:702
  23.1 7.2 %collective-permute-start.9 = (bf16[256,256]{1,0:T(8,128)(2,1)S(1)}, bf16[256,256]{1,0:T(8,128)(2,1)S(1)}, u32[]{:S(2)}, u32[]{:S(2)}) collective-permute-start(bf16[256,256]{1,0:T(8,128)(2,1)S(1)} %collective-permute-done.7.refs_9_), channel_id=1, source_target_pairs={{0,2},{1,3},{2,4},{3,5},{4,6},{5,7},{6,0},{7,1},{8,10},{9,11},{10,... | collective-permute-start | bytes 393224 | tf_op jit(solution)/shard_map/ppermute | solution.py:702
  23.5 8.0 %collective-permute-start.2 = (bf16[256,256]{1,0:T(8,128)(2,1)S(1)}, bf16[256,256]{1,0:T(8,128)(2,1)S(1)}, u32[]{:S(2)}, u32[]{:S(2)}) collective-permute-start(bf16[256,256]{1,0:T(8,128)(2,1)S(1)} %slice.4), channel_id=1, source_target_pairs={{0,2},{1,3},{2,4},{3,5},{4,6},{5,7},{6,0},{7,1},{8,10},{9,11},{10,... | collective-permute-start | bytes 393224 | tf_op jit(solution)/shard_map/ppermute | solution.py:702
  26.6 13.4 %collective-permute-start.4 = (bf16[320,256]{1,0:T(8,128)(2,1)S(1)}, bf16[320,256]{1,0:T(8,128)(2,1)S(1)}, u32[]{:S(2)}, u32[]{:S(2)}) collective-permute-start(bf16[320,256]{1,0:T(8,128)(2,1)S(1)} %collective-permute-done.refs_1_), channel_id=1, source_target_pairs={{0,1},{1,0},{2,3},{3,2},{4,5},{5,4},{6,7},{7,6},{8,9},{9,8},{10,11... | collective-permute-start | bytes 491528 | tf_op jit(solution)/shard_map/ppermute | solution.py:702
  28.1 15.1 %collective-permute-start.5 = (bf16[320,256]{1,0:T(8,128)(2,1)S(1)}, bf16[320,256]{1,0:T(8,128)(2,1)S(1)}, u32[]{:S(2)}, u32[]{:S(2)}) collective-permute-start(bf16[320,256]{1,0:T(8,128)(2,1)S(1)} %collective-permute-done.1.refs_2_), channel_id=1, source_target_pairs={{0,1},{1,0},{2,3},{3,2},{4,5},{5,4},{6,7},{7,6},{8,9},{9,8},{10,11... | collective-permute-start | bytes 491528 | tf_op jit(solution)/shard_map/ppermute | solution.py:702
  29.4 10.6 %collective-permute-start.11 = (bf16[256,256]{1,0:T(8,128)(2,1)S(1)}, bf16[256,256]{1,0:T(8,128)(2,1)S(1)}, u32[]{:S(2)}, u32[]{:S(2)}) collective-permute-start(bf16[256,256]{1,0:T(8,128)(2,1)S(1)} %collective-permute-done.7.refs_9_), channel_id=1, source_target_pairs={{0,1},{1,0},{2,3},{3,2},{4,5},{5,4},{6,7},{7,6},{8,9},{9,8},{10,11... | collective-permute-start | bytes 393224 | tf_op jit(solution)/shard_map/ppermute | solution.py:702
  30.3 11.5 %collective-permute-start.13 = (bf16[256,256]{1,0:T(8,128)(2,1)S(1)}, bf16[256,256]{1,0:T(8,128)(2,1)S(1)}, u32[]{:S(2)}, u32[]{:S(2)}) collective-permute-start(bf16[256,256]{1,0:T(8,128)(2,1)S(1)} %collective-permute-done.9.refs_11_), channel_id=1, source_target_pairs={{0,1},{1,0},{2,3},{3,2},{4,5},{5,4},{6,7},{7,6},{8,9},{9,8},{10,11... | collective-permute-start | bytes 393224 | tf_op jit(solution)/shard_map/ppermute | solution.py:702
  31.4 11.7 %collective-permute-start.6 = (bf16[256,256]{1,0:T(8,128)(2,1)S(1)}, bf16[256,256]{1,0:T(8,128)(2,1)S(1)}, u32[]{:S(2)}, u32[]{:S(2)}) collective-permute-start(bf16[256,256]{1,0:T(8,128)(2,1)S(1)} %collective-permute-done.2.refs_3_), channel_id=1, source_target_pairs={{0,1},{1,0},{2,3},{3,2},{4,5},{5,4},{6,7},{7,6},{8,9},{9,8},{10,11... | collective-permute-start | bytes 393224 | tf_op jit(solution)/shard_map/ppermute | solution.py:702
  47.9 3.1 %collective-permute-start.18 = (f32[16,128]{1,0:T(8,128)S(1)}, f32[16,128]{1,0:T(8,128)S(1)}, u32[]{:S(2)}, u32[]{:S(2)}) collective-permute-start(f32[16,128]{1,0:T(8,128)S(1)} %get-tuple-element.29.refs_0_), channel_id=1, source_target_pairs={{0,24},{8,16},{16,8},{24,0},{1,25},{9,17},{17,9},{25,1},{2,26},{10... | collective-permute-start | bytes 24584 | tf_op jit(solution)/shard_map/ppermute | solution.py:730
  48.0 3.7 %collective-permute-start.17 = (f32[16,128]{1,0:T(8,128)S(1)}, f32[16,128]{1,0:T(8,128)S(1)}, u32[]{:S(2)}, u32[]{:S(2)}) collective-permute-start(f32[16,128]{1,0:T(8,128)S(1)} %get-tuple-element.29.refs_0_), channel_id=1, source_target_pairs={{0,16},{8,24},{16,0},{24,8},{1,17},{9,25},{17,1},{25,9},{2,18},{10... | collective-permute-start | bytes 24584 | tf_op jit(solution)/shard_map/ppermute | solution.py:730
  49.6 2.1 %collective-permute-start.16 = (f32[16,128]{1,0:T(8,128)S(1)}, f32[16,128]{1,0:T(8,128)S(1)}, u32[]{:S(2)}, u32[]{:S(2)}) collective-permute-start(f32[16,128]{1,0:T(8,128)S(1)} %get-tuple-element.29.refs_0_), channel_id=1, source_target_pairs={{0,8},{8,0},{16,24},{24,16},{1,9},{9,1},{17,25},{25,17},{2,10},{10... | collective-permute-start | bytes 24584 | tf_op jit(solution)/shard_map/ppermute | solution.py:730
